TPU v7x, 32 devices: a whole 2x2x4 slice. The times are simulated.
32 devices in a mesh: seq: 16 (over z, x, core), fsdp: 2 (over y).
Axes of the slice: x: 2, y: 2, z: 4, core: 2. Of those that a mesh axis runs over, the one named last changes fastest.
Arguments:
- inputs: bfloat16 [2, 16384, 1024], P(None, 'seq', 'fsdp'), may hold values from -6 to 6
- first_factor: bfloat16 [128, 128, 128], P('seq'), may hold values from -0.5 to 0.5
- second_factor: bfloat16 [128, 128, 128], P('seq'), may hold values from -0.5 to 0.5
- gate_scale: float32 [1024], P('fsdp'), may hold values from -2 to 2
- gate_bias: float32 [1024], P('fsdp'), may hold values from -3 to 3
- in_weight: bfloat16 [1024, 4096], P('seq', 'fsdp'), may hold values from -0.1875 to 0.1875
- out_weight: bfloat16 [4096, 1024], P('fsdp', 'seq'), may hold values from -0.09375 to 0.09375
- cotangent: bfloat16 [2, 16384, 1024], P(None, 'seq', 'fsdp'), may hold values from -6 to 6
Outputs:
- result: bfloat16 [2, 16384, 1024], P(None, 'seq', 'fsdp')
- input_grad: bfloat16 [2, 16384, 1024], P(None, 'seq', 'fsdp')
- grad_in: float32 [1024, 4096], P('seq', 'fsdp')
- grad_out: float32 [4096, 1024], P('fsdp', 'seq')
All inputs are finite; a program needn't handle non-finite values.
Results may differ from a plain program's by a relative error of at most 0.0075.
Values may be sent and summed in bfloat16 or wider, within the bound.
A program may use at most 192 MiB of HBM per device.

v0:
```python
import jax
import jax.numpy as jnp
from jax import lax
from jax.sharding import PartitionSpec as P


def body(
    inputs, first_factor, second_factor, gate_scale, gate_bias, in_weight, out_weight, cotangent
):
    seq_count, tok_rows, chan_count = inputs.shape
    blocks = first_factor.shape[0]
    block_size = first_factor.shape[1]
    row_count = seq_count * tok_rows
    groups = lax.axis_size("fsdp")
    gate_gain = gate_scale.reshape(1, 1, 1, chan_count)
    gate_shift = gate_bias.reshape(1, 1, 1, chan_count)
    source = inputs.reshape(seq_count, blocks, block_size, chan_count)
    section_one = jnp.einsum(
        "mkn,smnc->smkc", first_factor, source, preferred_element_type=jnp.float32
    ).astype(jnp.bfloat16)
    turned, source_cols = (
        lax.all_to_all(section_one, "seq", split_axis=2, concat_axis=1, tiled=True),
        lax.all_to_all(source, "seq", split_axis=2, concat_axis=1, tiled=True),
    )
    section_two = jnp.einsum(
        "kjm,smkc->sjkc", second_factor, turned, preferred_element_type=jnp.float32
    ).astype(jnp.bfloat16)
    section_two = lax.optimization_barrier(section_two)
    gate_cols = jax.nn.sigmoid(gate_gain * source_cols.astype(jnp.float32) + gate_shift)
    gated_cols = (gate_cols * section_two.astype(jnp.float32)).astype(jnp.bfloat16)
    mixed_grid = lax.all_to_all(gated_cols, "seq", split_axis=1, concat_axis=2, tiled=True)
    mixed = mixed_grid.reshape(row_count, chan_count)
    full_in = lax.all_gather(in_weight, "seq", axis=0, tiled=True)
    full_out = lax.all_gather(out_weight, "seq", axis=1, tiled=True)
    mixed_all = lax.all_gather(mixed, "fsdp", axis=1, tiled=True)
    pre_act = jnp.dot(mixed_all, full_in, preferred_element_type=jnp.float32)
    hidden = jax.nn.silu(pre_act).astype(jnp.bfloat16)
    partial_out = jnp.dot(hidden, full_out, preferred_element_type=jnp.float32)
    received = lax.all_to_all(partial_out, "fsdp", split_axis=1, concat_axis=0, tiled=True)
    branch_sum = jnp.sum(received.reshape(groups, row_count, chan_count), axis=0)
    result = (
        (mixed.astype(jnp.float32) + branch_sum)
        .astype(jnp.bfloat16)
        .reshape(seq_count, tok_rows, chan_count)
    )
    upstream = cotangent.reshape(row_count, chan_count)
    upstream_all = lax.all_gather(upstream, "fsdp", axis=1, tiled=True)
    hidden_grad = lax.dot_general(
        upstream_all, full_out, (((1,), (1,)), ((), ())), preferred_element_type=jnp.float32
    )
    sigma = jax.nn.sigmoid(pre_act)
    pre_grad = (hidden_grad * sigma * (1.0 + pre_act * (1.0 - sigma))).astype(jnp.bfloat16)
    out_term = lax.dot_general(
        hidden, upstream_all, (((0,), (0,)), ((), ())), preferred_element_type=jnp.float32
    )
    grad_out = lax.psum_scatter(out_term, "seq", scatter_dimension=1, tiled=True) * (
        1.0 / block_size
    )
    in_term = lax.dot_general(
        mixed_all, pre_grad, (((0,), (0,)), ((), ())), preferred_element_type=jnp.float32
    )
    grad_in = lax.psum_scatter(in_term, "seq", scatter_dimension=0, tiled=True) * (1.0 / block_size)
    back_term = lax.dot_general(
        pre_grad, full_in, (((1,), (1,)), ((), ())), preferred_element_type=jnp.float32
    )
    back_pieces = lax.all_to_all(back_term, "fsdp", split_axis=1, concat_axis=0, tiled=True)
    back_sum = jnp.sum(back_pieces.reshape(groups, row_count, chan_count), axis=0)
    mixed_grad = (
        (upstream.astype(jnp.float32) + back_sum)
        .astype(jnp.bfloat16)
        .reshape(seq_count, blocks, block_size, chan_count)
    )
    grad_cols = lax.all_to_all(mixed_grad, "seq", split_axis=2, concat_axis=1, tiled=True).astype(
        jnp.float32
    )
    second_grad = (grad_cols * gate_cols).astype(jnp.bfloat16)
    gate_term = (
        grad_cols * section_two.astype(jnp.float32) * gate_cols * (1.0 - gate_cols) * gate_gain
    )
    gate_back = lax.all_to_all(
        gate_term.astype(jnp.bfloat16), "seq", split_axis=1, concat_axis=2, tiled=True
    ).astype(gate_term.dtype)
    first_grad = jnp.einsum(
        "kjm,sjkc->smkc", second_factor, second_grad, preferred_element_type=jnp.float32
    ).astype(jnp.bfloat16)
    first_rows = lax.all_to_all(first_grad, "seq", split_axis=1, concat_axis=2, tiled=True)
    input_sum = (
        jnp.einsum("mkn,smkc->smnc", first_factor, first_rows, preferred_element_type=jnp.float32)
        + gate_back
    )
    input_grad = input_sum.astype(jnp.bfloat16).reshape(seq_count, tok_rows, chan_count)
    return (result, input_grad, grad_in, grad_out)


def solution(mesh):
    in_specs = (
        P(None, "seq", "fsdp"),
        P("seq", None, None),
        P("seq", None, None),
        P("fsdp"),
        P("fsdp"),
        P("seq", "fsdp"),
        P("fsdp", "seq"),
        P(None, "seq", "fsdp"),
    )
    out_specs = (P(None, "seq", "fsdp"), P(None, "seq", "fsdp"), P("seq", "fsdp"), P("fsdp", "seq"))
    return jax.shard_map(body, mesh=mesh, in_specs=in_specs, out_specs=out_specs, check_vma=False)
```

profile of v0, /device:TPU:0, one launch (start us, length us, event | category | flops | bytes accessed | tf_op | source)
XLA Modules:
  0.0 822.4 jit_solution(12045572904759130662)
XLA Ops:
  7.2 4.2 copy.79
  11.4 7.4 all-to-all-start
  18.7 3.7 convert_bitcast_fusion.5
  22.4 6.2 copy.84
  28.6 31.2 %all-to-all-done = bf16[2,8,128,512]{3,1,0,2:T(8,128)(2,1)S(1)} async-done(((bf16[2,8,128,512]{3,1,0,2:T(8,128)(2,1)}), bf16[2,8,128,512]{3,1,0,2:T(8,128)(2,1)S(1)}, u32[]{:S(2)}, u32[]{:S(2)}) %all-to-all-start) | async-done | bytes 2097184 | tf_op jit(solution)/shard_map/all_to_all | solution.py:23
  59.8 11.3 %all-to-all-start.1 = ((bf16[2,8,128,512]{3,0,1,2:T(2,128)(2,1)}), bf16[2,8,128,512]{3,0,1,2:T(2,128)(2,1)}, u32[]{:S(2)}, u32[]{:S(2)}) async-start(bf16[2,8,128,512]{3,0,1,2:T(2,128)(2,1)} %copy.84), calls=%async_computation.1 | async-start | bytes 4194304 | tf_op jit(solution)/shard_map/all_to_all | solution.py:22
  73.1 2.6 copy.81
  75.7 5.3 copy.82
  81.1 39.6 %all-to-all-done.1 = bf16[2,8,128,512]{3,0,1,2:T(2,128)(2,1)} async-done(((bf16[2,8,128,512]{3,0,1,2:T(2,128)(2,1)}), bf16[2,8,128,512]{3,0,1,2:T(2,128)(2,1)}, u32[]{:S(2)}, u32[]{:S(2)}) %all-to-all-start.1) | async-done | bytes 2097184 | tf_op jit(solution)/shard_map/all_to_all | solution.py:22
  120.7 2.8 copy.132
  126.3 2.7 fusion
  129.1 5.0 copy.88
  134.1 73.4 %all_to_all.104 = bf16[2,128,8,512]{3,0,2,1:T(2,128)(2,1)S(1)} all-to-all(bf16[2,128,8,512]{3,0,2,1:T(2,128)(2,1)S(1)} %copy.88), channel_id=1, replica_groups=mesh['seq'=16,'fsdp'=2] {'seq'}, dimensions={1} | all-to-all | bytes 4194304 | tf_op jit(solution)/shard_map/all_to_all | solution.py:31
  212.6 55.4 %all-gather.5.cloned.1.call-done = bf16[2048,1024]{1,0:T(8,128)(2,1)} async-done(((bf16[2048,512]{1,0:T(8,128)(2,1)}), bf16[2048,1024]{1,0:T(8,128)(2,1)}) %all-gather.5.cloned.1.call-update) | async-done | bytes 4194320 | tf_op jit(solution)/shard_map/all_gather | solution.py:35
  268.0 18.4 %multiply_convert_fusion.1 = (bf16[2048,2048]{1,0:T(8,128)(2,1)}, f32[2048,2048]{1,0:T(8,128)}) fusion(bf16[2048,1024]{1,0:T(8,128)(2,1)} %all-gather.5.cloned.1.call-done, bf16[1024,2048]{1,0:T(8,128)(2,1)} %all-gather.7.cloned.1.call-done), kind=kOutput, calls=%fused_computation.1 | convolution fusion | flops 8610906112 | bytes 33554432 | tf_op jit(solution)/shard_map/dot_general | solution.py:36
  286.4 39.9 %all-gather.11.cloned.1.call-done = bf16[2048,1024]{1,0:T(8,128)(2,1)} async-done(((bf16[2048,512]{1,0:T(8,128)(2,1)}), bf16[2048,1024]{1,0:T(8,128)(2,1)}) %all-gather.11.cloned.1.call-update) | async-done | bytes 4194320 | tf_op jit(solution)/shard_map/all_gather | solution.py:47
  326.3 52.6 %all-gather.9.cloned.1.call-done = bf16[2048,1024]{0,1:T(8,128)(2,1)} async-done(((bf16[2048,64]{0,1:T(8,128)(2,1)}), bf16[2048,1024]{0,1:T(8,128)(2,1)}) %all-gather.9.cloned.1.call-update) | async-done | bytes 4194320 | tf_op jit(solution)/shard_map/all_gather | solution.py:34
  378.9 19.2 %multiply_convert_fusion = bf16[2048,2048]{1,0:T(8,128)(2,1)S(1)} fusion(f32[2048,2048]{1,0:T(8,128)} %get-tuple-element.5, bf16[2048,1024]{1,0:T(8,128)(2,1)} %all-gather.11.cloned.1.call-done, bf16[2048,1024]{0,1:T(8,128)(2,1)} %all-gather.9.cloned.1.call-done), kind=kOutput, calls=%fused_computation | convolution fusion | flops 8627683328 | bytes 33554432 | tf_op jit(solution)/shard_map/dot_general | solution.py:48
  398.1 3.2 copy-done.14
  401.3 11.4 %fusion.25 = f32[1024,2048]{1,0:T(8,128)} fusion(bf16[2048,1024]{1,0:T(8,128)(2,1)S(1)} %copy-done.13, bf16[2048,2048]{1,0:T(8,128)(2,1)S(1)} %multiply_convert_fusion), kind=kOutput, calls=%fused_computation.40 | convolution fusion | flops 8589934592 | bytes 20971520 | tf_op jit(solution)/shard_map/dot_general | solution.py:59
  412.8 12.6 %fusion.24 = f32[2048,1024]{0,1:T(8,128)S(1)} fusion(bf16[2048,2048]{1,0:T(8,128)(2,1)} %copy-done.14, bf16[1024,2048]{1,0:T(8,128)(2,1)} %all-gather.7.cloned.1.call-done), kind=kOutput, calls=%fused_computation.39 | convolution fusion | flops 8589934592 | bytes 20971520 | tf_op jit(solution)/shard_map/dot_general | solution.py:63
  425.3 97.4 %all_to_all.105 = f32[2048,2,512]{0,2,1:T(8,128)} all-to-all(f32[2048,2,512]{0,2,1:T(8,128)S(1)} %bitcast.96), channel_id=1, replica_groups=mesh['seq'=16,'fsdp'=2] {'fsdp'}, dimensions={1} | all-to-all | bytes 16777216 | tf_op jit(solution)/shard_map/all_to_all | solution.py:66
  522.7 6.6 reduce_sum.24
  529.3 5.5 copy.113
  534.9 2.9 fusion.5
  537.8 2.5 copy.94
  540.3 3.9 all-to-all-start.5
  544.2 14.7 %fusion.23 = f32[2048,1024]{0,1:T(8,128)} fusion(bf16[2048,2048]{1,0:T(8,128)(2,1)} %get-tuple-element.4, bf16[2048,1024]{0,1:T(8,128)(2,1)} %all-gather.9.cloned.1.call-done), kind=kOutput, calls=%fused_computation.38 | convolution fusion | flops 8589934592 | bytes 20971520 | tf_op jit(solution)/shard_map/dot_general | solution.py:38
  558.9 26.4 %all-to-all-done.5 = bf16[2,8,128,512]{3,1,0,2:T(8,128)(2,1)S(1)} async-done(((bf16[2,8,128,512]{3,1,0,2:T(8,128)(2,1)}), bf16[2,8,128,512]{3,1,0,2:T(8,128)(2,1)S(1)}, u32[]{:S(2)}, u32[]{:S(2)}) %all-to-all-start.5) | async-done | bytes 2097184 | tf_op jit(solution)/shard_map/all_to_all | solution.py:73
  585.2 7.0 all-to-all-start.3
  592.3 14.7 %fusion.26 = f32[2048,1024]{0,1:T(8,128)} fusion(bf16[2048,2048]{1,0:T(8,128)(2,1)} %get-tuple-element.4, bf16[2048,1024]{1,0:T(8,128)(2,1)} %all-gather.11.cloned.1.call-done), kind=kOutput, calls=%fused_computation.41 | convolution fusion | flops 8589934592 | bytes 20971520 | tf_op jit(solution)/shard_map/dot_general | solution.py:53
  608.2 2.6 copy.96
  610.8 5.5 copy.97
  616.3 5.8 fusion.4
  622.1 6.4 copy.103
  628.5 57.2 %all-to-all-done.3 = f32[2048,2,512]{0,2,1:T(8,128)} async-done(((f32[2048,2,512]{0,2,1:T(8,128)}), f32[2048,2,512]{0,2,1:T(8,128)}, u32[]{:S(2)}, u32[]{:S(2)}) %all-to-all-start.3) | async-done | bytes 8388640 | tf_op jit(solution)/shard_map/all_to_all | solution.py:39
  685.7 11.0 %all-to-all-start.7 = ((bf16[2,128,8,512]{3,0,2,1:T(2,128)(2,1)}), bf16[2,128,8,512]{3,0,2,1:T(2,128)(2,1)}, u32[]{:S(2)}, u32[]{:S(2)}) async-start(bf16[2,128,8,512]{3,0,2,1:T(2,128)(2,1)} %copy.103), calls=%async_computation.7 | async-start | bytes 4194304 | tf_op jit(solution)/shard_map/all_to_all | solution.py:80
  696.8 6.5 convert_bitcast_fusion.3
  703.3 6.4 copy.98
  709.7 45.0 %all-to-all-done.7 = bf16[2,128,8,512]{3,0,2,1:T(2,128)(2,1)} async-done(((bf16[2,128,8,512]{3,0,2,1:T(2,128)(2,1)}), bf16[2,128,8,512]{3,0,2,1:T(2,128)(2,1)}, u32[]{:S(2)}, u32[]{:S(2)}) %all-to-all-start.7) | async-done | bytes 2097184 | tf_op jit(solution)/shard_map/all_to_all | solution.py:80
  754.7 11.3 %all-to-all-start.6 = ((bf16[2,128,8,512]{3,0,2,1:T(2,128)(2,1)}), bf16[2,128,8,512]{3,0,2,1:T(2,128)(2,1)}, u32[]{:S(2)}, u32[]{:S(2)}) async-start(bf16[2,128,8,512]{3,0,2,1:T(2,128)(2,1)} %copy.98), calls=%async_computation.6 | async-start | bytes 4194304 | tf_op jit(solution)/shard_map/all_to_all | solution.py:86
  766.0 2.6 copy.90
  768.6 6.6 reduce_sum.22
  775.2 5.3 copy.112
  780.5 5.5 fusion.7
  786.1 2.0 copy.104
  788.0 19.2 %all-to-all-done.6 = bf16[2,128,8,512]{3,0,2,1:T(2,128)(2,1)} async-done(((bf16[2,128,8,512]{3,0,2,1:T(2,128)(2,1)}), bf16[2,128,8,512]{3,0,2,1:T(2,128)(2,1)}, u32[]{:S(2)}, u32[]{:S(2)}) %all-to-all-start.6) | async-done | bytes 2097184 | tf_op jit(solution)/shard_map/all_to_all | solution.py:86
  807.2 1.9 copy.99
  (54 shorter events, 17.2 us)
Async XLA Ops:
  7.2 116.5 %copy-start = (bf16[8,128,128]{2,1,0:T(8,128)(2,1)S(1)}, bf16[8,128,128]{2,1,0:T(8,128)(2,1)}, u32[]{:S(2)}) copy-start(bf16[8,128,128]{2,1,0:T(8,128)(2,1)} %param.10) | copy-start | bytes 786436
  7.2 11.5 %copy-start.7 = (bf16[8,128,128]{2,1,0:T(8,128)(2,1)S(1)}, bf16[8,128,128]{2,1,0:T(8,128)(2,1)}, u32[]{:S(2)}) copy-start(bf16[8,128,128]{2,1,0:T(8,128)(2,1)} %param.9) | copy-start | bytes 786436
  11.4 48.5 %all-to-all-start = ((bf16[2,8,128,512]{3,1,0,2:T(8,128)(2,1)}), bf16[2,8,128,512]{3,1,0,2:T(8,128)(2,1)S(1)}, u32[]{:S(2)}, u32[]{:S(2)}) async-start(bf16[2,8,128,512]{3,1,0,2:T(8,128)(2,1)} %copy.79), calls=%async_computation | async-start | bytes 4194304 | tf_op jit(solution)/shard_map/all_to_all | solution.py:23
  59.8 60.9 %all-to-all-start.1 = ((bf16[2,8,128,512]{3,0,1,2:T(2,128)(2,1)}), bf16[2,8,128,512]{3,0,1,2:T(2,128)(2,1)}, u32[]{:S(2)}, u32[]{:S(2)}) async-start(bf16[2,8,128,512]{3,0,1,2:T(2,128)(2,1)} %copy.84), calls=%async_computation.1 | async-start | bytes 4194304 | tf_op jit(solution)/shard_map/all_to_all | solution.py:22
  71.1 141.5 %all-gather.7.cloned.1.call-start = ((), (), s32[]{:S(2)}) async-start(), calls=%async_computation.11 | async-start | bytes 4456448 | tf_op jit(solution)/shard_map/all_gather | solution.py:33
  71.8 196.1 %all-gather.5.cloned.1.call-start = ((), (), s32[]{:S(2)}) async-start(), calls=%async_computation.10 | async-start | bytes 6291456 | tf_op jit(solution)/shard_map/all_gather | solution.py:35
  123.4 2.9 copy-start.1
  123.4 2.9 copy-start.9
  123.5 2.9 copy-start.11
  125.0 1.3 copy-start.4
  207.8 1.3 copy-start.2
  210.7 115.6 %all-gather.11.cloned.1.call-start = ((), (), s32[]{:S(2)}) async-start(), calls=%async_computation.13 | async-start | bytes 6291456 | tf_op jit(solution)/shard_map/all_gather | solution.py:47
  211.5 167.4 %all-gather.9.cloned.1.call-start = ((), (), s32[]{:S(2)}) async-start(), calls=%async_computation.12 | async-start | bytes 4456448 | tf_op jit(solution)/shard_map/all_gather | solution.py:34
  212.0 599.3 %reduce-scatter.3.cloned.1.call-start = ((), (), s32[]{:S(2)}) async-start(), calls=%async_computation.14 | async-start | bytes 8912896 | tf_op jit(solution)/shard_map/reduce_scatter | solution.py:62
  378.9 22.4 %copy-start.13 = (bf16[2048,1024]{1,0:T(8,128)(2,1)S(1)}, bf16[2048,1024]{1,0:T(8,128)(2,1)}, u32[]{:S(2)}) copy-start(bf16[2048,1024]{1,0:T(8,128)(2,1)} %all-gather.5.cloned.1.call-done) | copy-start | bytes 12582916
  398.1 3.3 copy-start.14
  529.3 5.5 copy-start.6
  540.3 45.0 %all-to-all-start.5 = ((bf16[2,8,128,512]{3,1,0,2:T(8,128)(2,1)}), bf16[2,8,128,512]{3,1,0,2:T(8,128)(2,1)S(1)}, u32[]{:S(2)}, u32[]{:S(2)}) async-start(bf16[2,8,128,512]{3,1,0,2:T(8,128)(2,1)} %copy.94), calls=%async_computation.5 | async-start | bytes 4194304 | tf_op jit(solution)/shard_map/all_to_all | solution.py:73
  585.2 100.5 %all-to-all-start.3 = ((f32[2048,2,512]{0,2,1:T(8,128)}), f32[2048,2,512]{0,2,1:T(8,128)}, u32[]{:S(2)}, u32[]{:S(2)}) async-start(f32[2048,2,512]{0,2,1:T(8,128)} %bitcast.95), calls=%async_computation.3 | async-start | bytes 16777216 | tf_op jit(solution)/shard_map/all_to_all | solution.py:39
  592.2 221.1 %reduce-scatter.5.cloned.1.call-start = ((), (), s32[]{:S(2)}) async-start(), calls=%async_computation.15 | async-start | bytes 8912896 | tf_op jit(solution)/shard_map/reduce_scatter | solution.py:56
  610.8 5.5 copy-start.5
  610.8 5.5 copy-start.10
  610.8 5.5 copy-start.12
  685.7 68.9 %all-to-all-start.7 = ((bf16[2,128,8,512]{3,0,2,1:T(2,128)(2,1)}), bf16[2,128,8,512]{3,0,2,1:T(2,128)(2,1)}, u32[]{:S(2)}, u32[]{:S(2)}) async-start(bf16[2,128,8,512]{3,0,2,1:T(2,128)(2,1)} %copy.103), calls=%async_computation.7 | async-start | bytes 4194304 | tf_op jit(solution)/shard_map/all_to_all | solution.py:80
  703.3 62.7 %copy-start.3 = (bf16[2,128,8,512]{3,2,1,0:T(8,128)(2,1)S(1)}, bf16[2,128,8,512]{3,2,1,0:T(8,128)(2,1)}, u32[]{:S(2)}) copy-start(bf16[2,128,8,512]{3,2,1,0:T(8,128)(2,1)} %copy-done.2) | copy-start | bytes 6291460
  754.7 52.5 %all-to-all-start.6 = ((bf16[2,128,8,512]{3,0,2,1:T(2,128)(2,1)}), bf16[2,128,8,512]{3,0,2,1:T(2,128)(2,1)}, u32[]{:S(2)}, u32[]{:S(2)}) async-start(bf16[2,128,8,512]{3,0,2,1:T(2,128)(2,1)} %copy.98), calls=%async_computation.6 | async-start | bytes 4194304 | tf_op jit(solution)/shard_map/all_to_all | solution.py:86
  786.0 23.1 %copy-start.8 = (bf16[8,128,128]{2,1,0:T(8,128)(2,1)S(1)}, bf16[8,128,128]{2,1,0:T(8,128)(2,1)}, u32[]{:S(2)}) copy-start(bf16[8,128,128]{2,1,0:T(8,128)(2,1)} %param.9) | copy-start | bytes 786436
Sparse Core Ops, SparseCore 0:
  74.1 72.9 all-gather.6
  210.8 57.0 all-gather.4
  269.5 56.7 all-gather.10
  328.3 50.5 all-gather.8
  412.9 103.0 reduce-scatter.2
  607.1 143.0 reduce-scatter.4
where the time goes:
time: 837 us; the launch traced here: 822 us
  waiting for transfers between devices  368 us (44%)
  blocking collectives  171 us (20%)
  matrix products  103 us (12%)
  local copies, waits for them, and re-layouts  76.3 us (9%)
  starting transfers between devices  52.5 us (6%)
  other arithmetic  36.3 us (4%)
  between operations  14.8 us (2%)
    all_to_all x1, blocking collectives, body(): lax.all_to_all(back_term, 'fsdp', split_axis=1, concat_axis=0, tiled=True)  97.4 us
    all_to_all x1, blocking collectives, body(): lax.all_to_all(gated_cols, 'seq', split_axis=1, concat_axis=2, tiled=True)  73.4 us
    all_to_all x1, waiting for transfers between devices, body(): lax.all_to_all(partial_out, 'fsdp', split_axis=1, concat_axis=0, tiled=True)  57.2 us
    all_gather x1, waiting for transfers between devices, body(): mixed_all = lax.all_gather(mixed, 'fsdp', axis=1, tiled=True)  55.4 us
    all_gather x1, waiting for transfers between devices, body(): full_out = lax.all_gather(out_weight, 'seq', axis=1, tiled=True)  52.6 us
    all_to_all x1, waiting for transfers between devices, body(): lax.all_to_all(gate_term.astype(jnp.bfloat16), 'seq', split_axis=1, conca...  45 us
    all_gather x1, waiting for transfers between devices, body(): upstream_all = lax.all_gather(upstream, 'fsdp', axis=1, tiled=True)  39.9 us
    all_to_all x1, waiting for transfers between devices, body(): lax.all_to_all(section_one, 'seq', split_axis=2, concat_axis=1, tiled=True)  39.6 us
  transfers between devices with their start and end apart: 12, of which 9 were waited for; matrix products, arithmetic and copies ran while one was open for 21% of the time, Pallas kernels for 0%

commit v1 on v0

v1 whole, which is shorter than its diff:
```python
import jax
import jax.numpy as jnp
from jax import lax
from jax.sharding import PartitionSpec as P

BF = jnp.bfloat16
F32 = jnp.float32


def body(
    inputs, first_factor, second_factor, gate_scale, gate_bias, in_weight, out_weight, cotangent
):
    seq_count, tok_rows, chan = inputs.shape
    blocks, size, _ = first_factor.shape
    offs = second_factor.shape[0]
    owners = lax.axis_size("seq")
    groups = lax.axis_size("fsdp")
    mine = lax.axis_index("fsdp")
    width = chan * groups
    gain = gate_scale.reshape(1, 1, chan)
    shift = gate_bias.reshape(1, 1, chan)

    def swap(x):
        return lax.ppermute(x, "fsdp", [(0, 1), (1, 0)])

    def gather_cols(x):
        if groups != 2:
            return lax.all_gather(x, "fsdp", axis=1, tiled=True)
        y = swap(x)
        first = mine == 0
        return jnp.concatenate([jnp.where(first, x, y), jnp.where(first, y, x)], axis=1)

    def reduce_cols(left, weight, dims):
        if groups != 2:
            full = lax.dot_general(left, weight, dims, preferred_element_type=F32)
            got = lax.all_to_all(full, "fsdp", split_axis=1, concat_axis=0, tiled=True)
            return jnp.sum(got.reshape(groups, -1, chan), axis=0), None
        other = lax.dynamic_slice_in_dim(weight, (1 - mine) * chan, chan, 0)
        own = lax.dynamic_slice_in_dim(weight, mine * chan, chan, 0)
        sent = swap(lax.dot_general(left, other, dims, preferred_element_type=F32).astype(BF))
        kept = lax.dot_general(left, own, dims, preferred_element_type=F32)
        return kept, sent

    def exchange(x):
        return lax.all_to_all(x, "seq", split_axis=0, concat_axis=0, tiled=True)

    def after(x, *others):
        return lax.optimization_barrier((x, *others))[0]

    def joined(pair, *others):
        kept, sent = pair
        if sent is None:
            return kept
        return kept + after(sent, *others).astype(F32)

    nt = (((1,), (1,)), ((), ()))
    tn = (((0,), (0,)), ((), ()))
    seqs = range(seq_count)
    last = seq_count - 1
    full_out = lax.all_gather(out_weight.T, "seq", axis=0, tiled=True)
    full_in = lax.all_gather(in_weight, "seq", axis=0, tiled=True)

    sources = [inputs[s].reshape(blocks, size, chan) for s in seqs]
    cots = [cotangent[s] for s in seqs]
    cot_all = [gather_cols(c) for c in cots]

    turned = []
    for s in seqs:
        u = jnp.einsum("mkn,mnc->mkc", first_factor, sources[s], preferred_element_type=F32)
        u = u.astype(BF).reshape(blocks, owners, offs, chan).transpose(1, 0, 2, 3)
        if s > 0:
            u = after(u, cot_all[s - 1])
        turned.append(exchange(u).reshape(owners * blocks, offs, chan))
    dhs = [jnp.dot(cot_all[s], full_out, preferred_element_type=F32) for s in seqs]
    mixes, seconds, mixed_all = [], [], []
    for s in seqs:
        w = jnp.einsum("kjm,mkc->kjc", second_factor, turned[s], preferred_element_type=F32)
        w = w.astype(BF).reshape(offs, owners, blocks, chan).transpose(1, 0, 2, 3)
        if s == 0:
            w = after(w, cot_all[last])
        w = after(exchange(w), *(dhs if s == 0 else mixed_all))
        w = w.reshape(size, blocks, chan).transpose(1, 0, 2)
        w = lax.optimization_barrier(w)
        gate = jax.nn.sigmoid(gain * sources[s].astype(F32) + shift)
        seconds.append(w)
        mixes.append((gate * w.astype(F32)).astype(BF).reshape(tok_rows, chan))
        mixed_all.append(gather_cols(mixes[s]))

    das, hs, sums = [], [], []
    for s in seqs:
        pre = jnp.dot(mixed_all[s], full_in, preferred_element_type=F32)
        sig = jax.nn.sigmoid(pre)
        hs.append((pre * sig).astype(BF))
        das.append((dhs[s] * sig * (1.0 + pre * (1.0 - sig))).astype(BF))
        sums.append(reduce_cols(das[s], full_in, nt))
    dms, dws, gates, sends = [], [], [], []
    for s in seqs:
        gate = jax.nn.sigmoid(gain * sources[s].astype(F32) + shift)
        dm = cots[s].astype(F32) + joined(sums[s], das[last], *sends)
        dm = dm.astype(BF).reshape(blocks, size, chan)
        dw = (dm.astype(F32) * gate).astype(BF)
        dw = dw.reshape(blocks, owners, offs, chan).transpose(1, 0, 2, 3)
        dms.append(dm)
        gates.append(gate)
        sends.append(dw)
        dws.append(exchange(dw))
    hs[0] = after(hs[0], sends[0])
    out_term = sum(lax.dot_general(cot_all[s], hs[s], tn, preferred_element_type=F32) for s in seqs)
    in_term = sum(lax.dot_general(mixed_all[s], das[s], tn, preferred_element_type=F32) for s in seqs)
    out_term, in_term = out_term.astype(BF), in_term.astype(BF)
    scale = 1.0 / size
    grad_out = lax.psum_scatter(out_term, "seq", scatter_dimension=0, tiled=True)
    grad_in = lax.psum_scatter(in_term, "seq", scatter_dimension=0, tiled=True)

    dws[0] = after(dws[0], out_term, in_term)
    branches = [reduce_cols(hs[s], full_out, nt) for s in seqs]
    if groups == 2:
        dws[last] = after(dws[last], branches[0][1])
    grads, results = [], []
    for s in seqs:
        dw = dws[s].reshape(owners * blocks, offs, chan)
        du = jnp.einsum("kjm,jkc->kmc", second_factor, dw, preferred_element_type=F32)
        du = du.astype(BF).reshape(offs, owners, blocks, chan).transpose(1, 0, 2, 3)
        du = exchange(du)
        du, kept = lax.optimization_barrier((du, branches[s][0]))
        du = du.reshape(size, blocks, chan)
        back = jnp.einsum("mkn,kmc->mnc", first_factor, du, preferred_element_type=F32)
        gate = gates[s]
        gate_term = dms[s].astype(F32) * seconds[s].astype(F32) * gate * (1.0 - gate) * gain
        grads.append((back + gate_term).astype(BF).reshape(tok_rows, chan))
        branch = kept if branches[s][1] is None else kept + branches[s][1].astype(F32)
        results.append((mixes[s].astype(F32) + branch).astype(BF))
    return (
        jnp.stack(results),
        jnp.stack(grads),
        grad_in.astype(F32) * scale,
        grad_out.astype(F32).T * scale,
    )


def solution(mesh):
    in_specs = (
        P(None, "seq", "fsdp"),
        P("seq", None, None),
        P("seq", None, None),
        P("fsdp"),
        P("fsdp"),
        P("seq", "fsdp"),
        P("fsdp", "seq"),
        P(None, "seq", "fsdp"),
    )
    out_specs = (P(None, "seq", "fsdp"), P(None, "seq", "fsdp"), P("seq", "fsdp"), P("fsdp", "seq"))
    return jax.shard_map(body, mesh=mesh, in_specs=in_specs, out_specs=out_specs, check_vma=False)
```

time: 837 us -> 475 us (0.57); the launches traced: 822 us -> 470 us
  blocking collectives: 171 us -> 0 us
  waiting for transfers between devices: 368 us -> 226 us
  local copies, waits for them, and re-layouts: 76.3 us -> 20.8 us
  matrix products: 103 us -> 116 us
  starting transfers between devices: 52.5 us -> 65.2 us
  other arithmetic: 36.3 us -> 27.4 us
    all_to_all x2 -> x0, blocking collectives: 171 us -> none  [the longest x1 97.4 us: body(): lax.all_to_all(back_term, 'fsdp', split_axis=1, concat_axis=0, tiled=True)]
    all_gather x3 -> x1, waiting for transfers between devices: 148 us -> 0.01 us  [body(): full_out = lax.all_gather(out_weight.T, 'seq', axis=0, tiled=True)]
    all_to_all x6 -> x8, waiting for transfers between devices: 219 us -> 143 us  [exchange(): return lax.all_to_all(x, 'seq', split_axis=0, concat_axis=0, tiled=True)]
    ppermute x0 -> x8, waiting for transfers between devices: none -> 65 us  [swap(): return lax.ppermute(x, 'fsdp', [(0, 1), (1, 0)])]
    convert_element_type x11 -> x0, local copies, waits for them, and re-layouts: 46.6 us -> none  [the longest x2 8.12 us: body(): lax.all_to_all(mixed_grad, 'seq', split_axis=2, concat_axis=1, tiled=True)]
    reduce_scatter x2, waiting for transfers between devices: 0.01 us -> 16.8 us  [the longest x1 16.8 us: body(): lax.psum_scatter(out_term, 'seq', scatter_dimension=0, tiled=True)]
    convert_element_type x6 -> x3, other arithmetic: 19.4 us -> 6.16 us  [the longest x2 3.44 us: body(): dw = (dm.astype(F32) * gate).astype(BF)]
    reduce_sum x2 -> x0, other arithmetic: 13.2 us -> none  [the longest x1 6.63 us: body(): jnp.sum(back_pieces.reshape(groups, row_count, chan_count), axis=0)]
  transfers between devices with their start and end apart: 12 -> 20, of which waited for: 9 -> 13; matrix products, arithmetic and copies ran while one was open for 21% -> 34% of each run, Pallas kernels for 0% -> 0%
where the time goes in v1:
time: 475 us; the launch traced here: 470 us
  waiting for transfers between devices  226 us (48%)
  matrix products  116 us (24%)
  starting transfers between devices  65.2 us (14%)
  other arithmetic  27.4 us (6%)
  local copies, waits for them, and re-layouts  20.8 us (4%)
  between operations  14.7 us (3%)
    all_to_all x8, waiting for transfers between devices, exchange(): return lax.all_to_all(x, 'seq', split_axis=0, concat_axis=0, tiled=True)  143 us
    ppermute x8, waiting for transfers between devices, swap(): return lax.ppermute(x, 'fsdp', [(0, 1), (1, 0)])  65 us
    all_to_all x8, starting transfers between devices, exchange(): return lax.all_to_all(x, 'seq', split_axis=0, concat_axis=0, tiled=True)  55.3 us
    dot_general x2, matrix products, body(): pre = jnp.dot(mixed_all[s], full_in, preferred_element_type=F32)  23.6 us
    dot_general x4, matrix products, reduce_cols(): lax.dot_general(left, other, dims, preferred_element_type=F32).astype(BF)  18.8 us
    dot_general x2, matrix products, body(): lax.dot_general(cot_all[s], hs[s], tn, preferred_element_type=F32)  18.4 us
    dot_general x2, matrix products, body(): jnp.dot(cot_all[s], full_out, preferred_element_type=F32)  17.5 us
    reduce_scatter x1, waiting for transfers between devices, body(): lax.psum_scatter(out_term, 'seq', scatter_dimension=0, tiled=True)  16.8 us
  transfers between devices with their start and end apart: 20, of which 13 were waited for; matrix products, arithmetic and copies ran while one was open for 34% of the time, Pallas kernels for 0%

profile of v1, /device:TPU:0, one launch (start us, length us, event | category | flops | bytes accessed | tf_op | source)
XLA Modules:
  0.0 469.9 jit_solution(18252983504790245486)
XLA Ops:
  11.2 7.4 %all-to-all-start.2 = ((bf16[16,8,8,512]{3,2,1,0:T(8,128)(2,1)}), bf16[16,8,8,512]{3,2,1,0:T(8,128)(2,1)S(1)}, u32[]{:S(2)}, u32[]{:S(2)}) async-start(bf16[16,8,8,512]{3,2,1,0:T(8,128)(2,1)} %bitcast.131), calls=%async_computation.2 | async-start | bytes 2097152 | tf_op jit(solution)/shard_map/all_to_all | solution.py:45
  20.1 29.8 %all-to-all-done.2 = bf16[16,8,8,512]{3,2,1,0:T(8,128)(2,1)S(1)} async-done(((bf16[16,8,8,512]{3,2,1,0:T(8,128)(2,1)}), bf16[16,8,8,512]{3,2,1,0:T(8,128)(2,1)S(1)}, u32[]{:S(2)}, u32[]{:S(2)}) %all-to-all-start.2) | async-done | bytes 1048608 | tf_op jit(solution)/shard_map/all_to_all | solution.py:45
  49.9 6.9 %all-to-all-start = ((bf16[16,8,8,512]{3,2,1,0:T(8,128)(2,1)}), bf16[16,8,8,512]{3,2,1,0:T(8,128)(2,1)}, u32[]{:S(2)}, u32[]{:S(2)}) async-start(bf16[16,8,8,512]{3,2,1,0:T(8,128)(2,1)} %bitcast.134), calls=%async_computation | async-start | bytes 2097152 | tf_op jit(solution)/shard_map/all_to_all | solution.py:45
  60.0 32.0 %all-to-all-done = bf16[16,8,8,512]{3,2,1,0:T(8,128)(2,1)} async-done(((bf16[16,8,8,512]{3,2,1,0:T(8,128)(2,1)}), bf16[16,8,8,512]{3,2,1,0:T(8,128)(2,1)}, u32[]{:S(2)}, u32[]{:S(2)}) %all-to-all-start) | async-done | bytes 1048608 | tf_op jit(solution)/shard_map/all_to_all | solution.py:45
  91.9 6.8 %all-to-all-start.3 = ((bf16[16,8,8,512]{3,1,2,0:T(8,128)(2,1)}), bf16[16,8,8,512]{3,1,2,0:T(8,128)(2,1)}, u32[]{:S(2)}, u32[]{:S(2)}) async-start(bf16[16,8,8,512]{3,1,2,0:T(8,128)(2,1)} %bitcast.150), calls=%async_computation.3 | async-start | bytes 2097152 | tf_op jit(solution)/shard_map/all_to_all | solution.py:45
  102.2 2.0 fusion.58
  105.8 24.3 %all-to-all-done.3 = bf16[16,8,8,512]{3,1,2,0:T(8,128)(2,1)} async-done(((bf16[16,8,8,512]{3,1,2,0:T(8,128)(2,1)}), bf16[16,8,8,512]{3,1,2,0:T(8,128)(2,1)}, u32[]{:S(2)}, u32[]{:S(2)}) %all-to-all-start.3) | async-done | bytes 1048608 | tf_op jit(solution)/shard_map/all_to_all | solution.py:45
  130.1 6.9 %all-to-all-start.1 = ((bf16[16,8,8,512]{3,1,2,0:T(8,128)(2,1)}), bf16[16,8,8,512]{3,1,2,0:T(8,128)(2,1)}, u32[]{:S(2)}, u32[]{:S(2)}) async-start(bf16[16,8,8,512]{3,1,2,0:T(8,128)(2,1)} %bitcast.149), calls=%async_computation.1 | async-start | bytes 2097152 | tf_op jit(solution)/shard_map/all_to_all | solution.py:45
  137.3 11.1 %collective-permute-done = bf16[1024,512]{1,0:T(8,128)(2,1)} collective-permute-done((bf16[1024,512]{1,0:T(8,128)(2,1)}, bf16[1024,512]{1,0:T(8,128)(2,1)}, u32[]{:S(2)}, u32[]{:S(2)}) %collective-permute-start) | collective-permute-done | bytes 1048608 | tf_op jit(solution)/shard_map/ppermute | solution.py:24
  148.4 3.7 broadcast_select_fusion.5
  152.1 2.3 copy.94
  154.4 10.9 %fusion.87 = f32[1024,2048]{1,0:T(8,128)} fusion(bf16[1024,2048]{1,0:T(8,128)(2,1)} %all-gather.3.cloned.1.call-done, bf16[1024,512]{1,0:T(8,128)(2,1)} %get-tuple-element.35, bf16[1024,512]{1,0:T(8,128)(2,1)} %get-tuple-element.34), kind=kOutput, calls=%fused_computation.131 | convolution fusion | flops 4299161600 | bytes 14680064 | tf_op jit(solution)/shard_map/dot_general | solution.py:74
  165.3 6.6 %fusion.89 = f32[1024,2048]{1,0:T(8,128)} fusion(bf16[1024,2048]{1,0:T(8,128)(2,1)S(1)} %copy-done.31, bf16[1024,512]{1,0:T(8,128)(2,1)S(1)} %copy-done.19, bf16[1024,512]{1,0:T(8,128)(2,1)S(1)} %copy-done.21), kind=kOutput, calls=%fused_computation.133 | convolution fusion | flops 4299161600 | bytes 14680064 | tf_op jit(solution)/shard_map/dot_general | solution.py:74
  174.0 2.7 fusion
  178.7 24.3 %collective-permute-done.4 = bf16[1024,512]{1,0:T(8,128)(2,1)} collective-permute-done((bf16[1024,512]{1,0:T(8,128)(2,1)}, bf16[1024,512]{1,0:T(8,128)(2,1)}, u32[]{:S(2)}, u32[]{:S(2)}) %collective-permute-start.4) | collective-permute-done | bytes 1048608 | tf_op jit(solution)/shard_map/ppermute | solution.py:24
  203.0 3.1 broadcast_select_fusion.1
  206.1 12.8 %multiply_convert_fusion = (bf16[1024,2048]{1,0:T(8,128)(2,1)}, bf16[1024,2048]{1,0:T(8,128)(2,1)S(1)}) fusion(f32[1024,2048]{1,0:T(8,128)} %fusion.89, bf16[1024,2048]{1,0:T(8,128)(2,1)} %all-gather.5.cloned.1.call-done, bf16[1024,512]{1,0:T(8,128)(2,1)} %get-tuple-element.47, bf16[1024,512]{1,0:T(8,128)(2,1)} %get-tuple-element.46), kind=kOutput, calls=%fused_computation.2 | convolution fusion | flops 4322230272 | bytes 23068672 | tf_op jit(solution)/shard_map/dot_general | solution.py:91
  219.0 3.4 fusion.45
  224.0 4.6 fusion.60
  229.9 10.8 %multiply_convert_fusion.1 = (bf16[1024,2048]{1,0:T(8,128)(2,1)}, bf16[1024,2048]{1,0:T(8,128)(2,1)S(1)}) fusion(f32[1024,2048]{1,0:T(8,128)} %fusion.87, bf16[1024,2048]{1,0:T(8,128)(2,1)S(1)} %copy-done.33, bf16[1024,512]{1,0:T(8,128)(2,1)S(1)} %get-tuple-element.39, bf16[1024,512]{1,0:T(8,128)(2,1)S(1)} %get-tuple-element.38), kind=kOutput, calls=%fused_computation.3 | convolution fusion | flops 4322230272 | bytes 23068672 | tf_op jit(solution)/shard_map/dot_general | solution.py:91
  240.7 3.4 fusion.42
  244.5 6.4 %add_convert_fusion = bf16[1024,2048]{1,0:T(8,128)(2,1)} fusion(f32[1024,2048]{1,0:T(8,128)S(1)} %fusion.60, bf16[1024,2048]{1,0:T(8,128)(2,1)S(1)} %get-tuple-element.33, bf16[1024,512]{1,0:T(8,128)(2,1)S(1)} %get-tuple-element.39, bf16[1024,512]{1,0:T(8,128)(2,1)S(1)} %get-tuple-element.38), kind=kOutput, calls=%fused_computation | convolution fusion | flops 4303355904 | bytes 18874368 | tf_op jit(solution)/shard_map/dot_general | solution.py:109
  250.9 5.4 %fusion.40 = f32[1024,512]{1,0:T(8,128)S(1)} fusion(bf16[1024,2048]{1,0:T(8,128)(2,1)} %copy-done.40, bf16[1024,2048]{1,0:T(8,128)(2,1)} %all-gather.5.cloned.1.call-done, s32[]{:T(128)S(6)} %select_n.55), kind=kOutput, calls=%fused_computation.66 | convolution fusion | flops 2147483648 | bytes 8388612 | tf_op jit(solution)/shard_map/dot_general | solution.py:41
  256.3 2.4 fusion.38
  258.7 10.9 %collective-permute-done.3 = bf16[1024,512]{1,0:T(8,128)(2,1)} collective-permute-done((bf16[1024,512]{1,0:T(8,128)(2,1)}, bf16[1024,512]{1,0:T(8,128)(2,1)}, u32[]{:S(2)}, u32[]{:S(2)}) %collective-permute-start.3) | collective-permute-done | bytes 1048608 | tf_op jit(solution)/shard_map/ppermute | solution.py:24
  274.3 1.7 fusion.64
  278.5 6.7 %all-to-all-start.6 = ((bf16[16,8,8,512]{3,2,1,0:T(8,128)(2,1)}), bf16[16,8,8,512]{3,2,1,0:T(8,128)(2,1)S(1)}, u32[]{:S(2)}, u32[]{:S(2)}) async-start(bf16[16,8,8,512]{3,2,1,0:T(8,128)(2,1)} %copy.56), calls=%async_computation.6 | async-start | bytes 2097152 | tf_op jit(solution)/shard_map/all_to_all | solution.py:45
  286.4 34.6 %all-to-all-done.6 = bf16[16,8,8,512]{3,2,1,0:T(8,128)(2,1)S(1)} async-done(((bf16[16,8,8,512]{3,2,1,0:T(8,128)(2,1)}), bf16[16,8,8,512]{3,2,1,0:T(8,128)(2,1)S(1)}, u32[]{:S(2)}, u32[]{:S(2)}) %all-to-all-start.6) | async-done | bytes 1048608 | tf_op jit(solution)/shard_map/all_to_all | solution.py:45
  320.9 7.6 %all-to-all-start.4 = ((bf16[16,8,8,512]{3,2,1,0:T(8,128)(2,1)}), bf16[16,8,8,512]{3,2,1,0:T(8,128)(2,1)S(1)}, u32[]{:S(2)}, u32[]{:S(2)}) async-start(bf16[16,8,8,512]{3,2,1,0:T(8,128)(2,1)} %copy.52), calls=%async_computation.4 | async-start | bytes 2097152 | tf_op jit(solution)/shard_map/all_to_all | solution.py:45
  328.6 5.4 %fusion.48 = bf16[1024,512]{1,0:T(8,128)(2,1)S(1)} fusion(bf16[1024,2048]{1,0:T(8,128)(2,1)} %get-tuple-element.22, bf16[1024,2048]{1,0:T(8,128)(2,1)} %all-gather.3.cloned.1.call-done, s32[]{:T(128)S(6)} %select_n.56), kind=kOutput, calls=%fused_computation.70 | convolution fusion | flops 2148007936 | bytes 7340036 | tf_op jit(solution)/shard_map/dot_general | solution.py:40
  333.9 1.8 collective-permute-start.5
  335.7 6.8 %fusion.88 = f32[1024,2048]{1,0:T(8,128)} fusion(bf16[1024,2048]{1,0:T(8,128)(2,1)S(1)} %copy-done.35, bf16[1024,512]{1,0:T(8,128)(2,1)S(1)} %copy-done.20, bf16[1024,512]{1,0:T(8,128)(2,1)S(1)} %copy-done.22), kind=kOutput, calls=%fused_computation.132 | convolution fusion | flops 4299161600 | bytes 14680064 | tf_op jit(solution)/shard_map/dot_general | solution.py:108
  342.6 17.0 %collective-permute-done.5 = bf16[1024,512]{1,0:T(8,128)(2,1)S(1)} collective-permute-done((bf16[1024,512]{1,0:T(8,128)(2,1)S(1)}, bf16[1024,512]{1,0:T(8,128)(2,1)S(1)}, u32[]{:S(2)}, u32[]{:S(2)}) %collective-permute-start.5) | collective-permute-done | bytes 1048608 | tf_op jit(solution)/shard_map/ppermute | solution.py:24
  361.6 5.8 %all-to-all-start.7 = ((bf16[16,8,8,512]{3,2,1,0:T(8,128)(2,1)}), bf16[16,8,8,512]{3,2,1,0:T(8,128)(2,1)}, u32[]{:S(2)}, u32[]{:S(2)}) async-start(bf16[16,8,8,512]{3,2,1,0:T(8,128)(2,1)} %bitcast.127), calls=%async_computation.7 | async-start | bytes 2097152 | tf_op jit(solution)/shard_map/all_to_all | solution.py:45
  367.5 11.5 %add_convert_fusion.1 = bf16[1024,2048]{1,0:T(8,128)(2,1)} fusion(f32[1024,2048]{1,0:T(8,128)} %fusion.88, bf16[1024,2048]{1,0:T(8,128)(2,1)} %get-tuple-element.22, bf16[1024,512]{1,0:T(8,128)(2,1)} %get-tuple-element.35, bf16[1024,512]{1,0:T(8,128)(2,1)S(1)} %copy-done.18), kind=kOutput, calls=%fused_computation.1 | convolution fusion | flops 4303355904 | bytes 18874368 | tf_op jit(solution)/shard_map/dot_general | solution.py:108
  381.0 9.4 %all-to-all-done.7 = bf16[16,8,8,512]{3,2,1,0:T(8,128)(2,1)} async-done(((bf16[16,8,8,512]{3,2,1,0:T(8,128)(2,1)}), bf16[16,8,8,512]{3,2,1,0:T(8,128)(2,1)}, u32[]{:S(2)}, u32[]{:S(2)}) %all-to-all-start.7) | async-done | bytes 1048608 | tf_op jit(solution)/shard_map/all_to_all | solution.py:45
  390.5 7.2 %all-to-all-start.5 = ((bf16[16,8,8,512]{3,2,1,0:T(8,128)(2,1)}), bf16[16,8,8,512]{3,2,1,0:T(8,128)(2,1)}, u32[]{:S(2)}, u32[]{:S(2)}) async-start(bf16[16,8,8,512]{3,2,1,0:T(8,128)(2,1)} %bitcast.128), calls=%async_computation.5 | async-start | bytes 2097152 | tf_op jit(solution)/shard_map/all_to_all | solution.py:45
  397.7 6.7 %fusion.51 = bf16[1024,512]{1,0:T(8,128)(2,1)} fusion(bf16[1024,2048]{1,0:T(8,128)(2,1)} %get-tuple-element.30, bf16[1024,2048]{1,0:T(8,128)(2,1)} %all-gather.3.cloned.1.call-done, s32[]{:T(128)S(6)} %select_n.56), kind=kOutput, calls=%fused_computation.71 | convolution fusion | flops 2148007936 | bytes 7340036 | tf_op jit(solution)/shard_map/dot_general | solution.py:40
  406.1 3.7 fusion.30
  409.8 3.7 fusion.32
  413.5 12.8 %all-to-all-done.5 = bf16[16,8,8,512]{3,2,1,0:T(8,128)(2,1)} async-done(((bf16[16,8,8,512]{3,2,1,0:T(8,128)(2,1)}), bf16[16,8,8,512]{3,2,1,0:T(8,128)(2,1)}, u32[]{:S(2)}, u32[]{:S(2)}) %all-to-all-start.5) | async-done | bytes 1048608 | tf_op jit(solution)/shard_map/all_to_all | solution.py:45
  426.3 2.2 fusion.63
  430.2 2.1 fusion.65
  435.3 2.9 fusion.11
  438.2 2.8 fusion.5
  442.6 1.8 convert_multiply_fusion.6
  444.4 16.8 %reduce-scatter.5.cloned.1.call-done = bf16[64,2048]{1,0:T(8,128)(2,1)} async-done(((bf16[1024,2048]{1,0:T(8,128)(2,1)}), bf16[64,2048]{1,0:T(8,128)(2,1)}) %reduce-scatter.5.cloned.1.call-update) | async-done | bytes 262160 | tf_op jit(solution)/shard_map/reduce_scatter | solution.py:112
  461.1 1.8 multiply_bitcast_fusion
  (128 shorter events, 41.6 us)
Async XLA Ops:
  7.2 50.4 %copy-start = (bf16[8,128,128]{2,1,0:T(8,128)(2,1)S(1)}, bf16[8,128,128]{2,1,0:T(8,128)(2,1)}, u32[]{:S(2)}) copy-start(bf16[8,128,128]{2,1,0:T(8,128)(2,1)} %param.10) | copy-start | bytes 786436
  7.2 147.2 %all-gather.3.cloned.1.call-start = ((), (), s32[]{:S(2)}) async-start(), calls=%async_computation.10 | async-start | bytes 4456448 | tf_op jit(solution)/shard_map/all_gather | solution.py:60
  11.2 38.7 %all-to-all-start.2 = ((bf16[16,8,8,512]{3,2,1,0:T(8,128)(2,1)}), bf16[16,8,8,512]{3,2,1,0:T(8,128)(2,1)S(1)}, u32[]{:S(2)}, u32[]{:S(2)}) async-start(bf16[16,8,8,512]{3,2,1,0:T(8,128)(2,1)} %bitcast.131), calls=%async_computation.2 | async-start | bytes 2097152 | tf_op jit(solution)/shard_map/all_to_all | solution.py:45
  49.9 42.1 %all-to-all-start = ((bf16[16,8,8,512]{3,2,1,0:T(8,128)(2,1)}), bf16[16,8,8,512]{3,2,1,0:T(8,128)(2,1)}, u32[]{:S(2)}, u32[]{:S(2)}) async-start(bf16[16,8,8,512]{3,2,1,0:T(8,128)(2,1)} %bitcast.134), calls=%async_computation | async-start | bytes 2097152 | tf_op jit(solution)/shard_map/all_to_all | solution.py:45
  56.8 149.4 %all-gather.5.cloned.1.call-start = ((), (), s32[]{:S(2)}) async-start(), calls=%async_computation.11 | async-start | bytes 4456448 | tf_op jit(solution)/shard_map/all_gather | solution.py:61
  58.4 40.3 %copy-start.1 = (bf16[2,1024,512]{2,1,0:T(8,128)(2,1)S(1)}, bf16[2,1024,512]{2,1,0:T(8,128)(2,1)}, u32[]{:S(2)}) copy-start(bf16[2,1024,512]{2,1,0:T(8,128)(2,1)} %param.15) | copy-start | bytes 6291460
  91.9 38.1 %all-to-all-start.3 = ((bf16[16,8,8,512]{3,1,2,0:T(8,128)(2,1)}), bf16[16,8,8,512]{3,1,2,0:T(8,128)(2,1)}, u32[]{:S(2)}, u32[]{:S(2)}) async-start(bf16[16,8,8,512]{3,1,2,0:T(8,128)(2,1)} %bitcast.150), calls=%async_computation.3 | async-start | bytes 2097152 | tf_op jit(solution)/shard_map/all_to_all | solution.py:45
  100.2 37.1 %collective-permute-start.1 = (bf16[1024,512]{1,0:T(8,128)(2,1)}, bf16[1024,512]{1,0:T(8,128)(2,1)}, u32[]{:S(2)}, u32[]{:S(2)}) collective-permute-start(bf16[1024,512]{1,0:T(8,128)(2,1)} %get-tuple-element.42), channel_id=1, source_target_pairs={{0,1},{1,0},{2,3},{3,2},{4,5},{5,4},{6,7},{7,6},{8,9},{9,8},{10,11... | collective-permute-start | bytes 3145736 | tf_op jit(solution)/shard_map/ppermute | solution.py:24
  101.9 46.5 %collective-permute-start = (bf16[1024,512]{1,0:T(8,128)(2,1)}, bf16[1024,512]{1,0:T(8,128)(2,1)}, u32[]{:S(2)}, u32[]{:S(2)}) collective-permute-start(bf16[1024,512]{1,0:T(8,128)(2,1)} %get-tuple-element.43), channel_id=1, source_target_pairs={{0,1},{1,0},{2,3},{3,2},{4,5},{5,4},{6,7},{7,6},{8,9},{9,8},{10,11... | collective-permute-start | bytes 3145736 | tf_op jit(solution)/shard_map/ppermute | solution.py:24
  130.1 42.0 %all-to-all-start.1 = ((bf16[16,8,8,512]{3,1,2,0:T(8,128)(2,1)}), bf16[16,8,8,512]{3,1,2,0:T(8,128)(2,1)}, u32[]{:S(2)}, u32[]{:S(2)}) async-start(bf16[16,8,8,512]{3,1,2,0:T(8,128)(2,1)} %bitcast.149), calls=%async_computation.1 | async-start | bytes 2097152 | tf_op jit(solution)/shard_map/all_to_all | solution.py:45
  137.0 305.6 %reduce-scatter.3.cloned.1.call-start = ((), (), s32[]{:S(2)}) async-start(), calls=%async_computation.12 | async-start | bytes 4456448 | tf_op jit(solution)/shard_map/reduce_scatter | solution.py:113
  154.4 10.9 %copy-start.19 = (bf16[1024,512]{1,0:T(8,128)(2,1)S(1)}, bf16[1024,512]{1,0:T(8,128)(2,1)}, u32[]{:S(2)}) copy-start(bf16[1024,512]{1,0:T(8,128)(2,1)} %get-tuple-element.40) | copy-start | bytes 3145732
  154.4 10.9 %copy-start.21 = (bf16[1024,512]{1,0:T(8,128)(2,1)S(1)}, bf16[1024,512]{1,0:T(8,128)(2,1)}, u32[]{:S(2)}) copy-start(bf16[1024,512]{1,0:T(8,128)(2,1)} %get-tuple-element.41) | copy-start | bytes 3145732
  154.4 10.9 %copy-start.31 = (bf16[1024,2048]{1,0:T(8,128)(2,1)S(1)}, bf16[1024,2048]{1,0:T(8,128)(2,1)}, u32[]{:S(2)}) copy-start(bf16[1024,2048]{1,0:T(8,128)(2,1)} %all-gather.3.cloned.1.call-done) | copy-start | bytes 12582916
  165.3 8.3 %copy-start.29 = (f32[512]{0:T(512)S(1)}, f32[512]{0:T(512)}, u32[]{:S(2)}) copy-start(f32[512]{0:T(512)} %param.12) | copy-start | bytes 6148
  165.3 8.3 %copy-start.30 = (f32[512]{0:T(512)S(1)}, f32[512]{0:T(512)}, u32[]{:S(2)}) copy-start(f32[512]{0:T(512)} %param.11) | copy-start | bytes 6148
  173.6 3.1 copy-start.15
  176.7 26.3 %collective-permute-start.4 = (bf16[1024,512]{1,0:T(8,128)(2,1)}, bf16[1024,512]{1,0:T(8,128)(2,1)}, u32[]{:S(2)}, u32[]{:S(2)}) collective-permute-start(bf16[1024,512]{1,0:T(8,128)(2,1)} %bitcast.22), channel_id=1, source_target_pairs={{0,1},{1,0},{2,3},{3,2},{4,5},{5,4},{6,7},{7,6},{8,9},{9,8},{10,11... | collective-permute-start | bytes 3145736 | tf_op jit(solution)/shard_map/ppermute | solution.py:24
  178.3 50.3 %collective-permute-start.2 = (bf16[1024,512]{1,0:T(8,128)(2,1)}, bf16[1024,512]{1,0:T(8,128)(2,1)}, u32[]{:S(2)}, u32[]{:S(2)}) collective-permute-start(bf16[1024,512]{1,0:T(8,128)(2,1)} %bitcast.143), channel_id=1, source_target_pairs={{0,1},{1,0},{2,3},{3,2},{4,5},{5,4},{6,7},{7,6},{8,9},{9,8},{10,11... | collective-permute-start | bytes 3145736 | tf_op jit(solution)/shard_map/ppermute | solution.py:24
  206.1 12.8 %copy-start.33 = (bf16[1024,2048]{1,0:T(8,128)(2,1)S(1)}, bf16[1024,2048]{1,0:T(8,128)(2,1)}, u32[]{:S(2)}) copy-start(bf16[1024,2048]{1,0:T(8,128)(2,1)} %all-gather.5.cloned.1.call-done) | copy-start | bytes 12582916
  219.0 5.0 %copy-start.37 = (bf16[1024,2048]{1,0:T(8,128)(2,1)}, bf16[1024,2048]{1,0:T(8,128)(2,1)S(1)}, u32[]{:S(2)}) copy-start(bf16[1024,2048]{1,0:T(8,128)(2,1)S(1)} %get-tuple-element.31) | copy-start | bytes 12582916
  219.0 5.0 %copy-start.25 = (bf16[1024,512]{1,0:T(8,128)(2,1)S(1)}, bf16[1024,512]{1,0:T(8,128)(2,1)}, u32[]{:S(2)}) copy-start(bf16[1024,512]{1,0:T(8,128)(2,1)} %get-tuple-element.46) | copy-start | bytes 3145732
  219.0 5.0 %copy-start.26 = (bf16[1024,512]{1,0:T(8,128)(2,1)S(1)}, bf16[1024,512]{1,0:T(8,128)(2,1)}, u32[]{:S(2)}) copy-start(bf16[1024,512]{1,0:T(8,128)(2,1)} %get-tuple-element.47) | copy-start | bytes 3145732
  222.4 6.2 %copy-start.6 = (bf16[8,128,512]{2,1,0:T(8,128)(2,1)S(1)}, bf16[8,128,512]{2,1,0:T(8,128)(2,1)}, u32[]{:S(2)}) copy-start(bf16[8,128,512]{2,1,0:T(8,128)(2,1)} %get-tuple-element.48) | copy-start | bytes 3145732
  222.4 51.9 %collective-permute-start.6 = (bf16[1024,512]{1,0:T(8,128)(2,1)}, bf16[1024,512]{1,0:T(8,128)(2,1)}, u32[]{:S(2)}, u32[]{:S(2)}) collective-permute-start(bf16[1024,512]{1,0:T(8,128)(2,1)} %fusion.45), channel_id=1, source_target_pairs={{0,1},{1,0},{2,3},{3,2},{4,5},{5,4},{6,7},{7,6},{8,9},{9,8},{10,11... | collective-permute-start | bytes 3145736 | tf_op jit(solution)/shard_map/ppermute | solution.py:24
  240.7 3.8 copy-start.40
  244.0 25.6 %collective-permute-start.3 = (bf16[1024,512]{1,0:T(8,128)(2,1)}, bf16[1024,512]{1,0:T(8,128)(2,1)}, u32[]{:S(2)}, u32[]{:S(2)}) collective-permute-start(bf16[1024,512]{1,0:T(8,128)(2,1)} %fusion.42), channel_id=1, source_target_pairs={{0,1},{1,0},{2,3},{3,2},{4,5},{5,4},{6,7},{7,6},{8,9},{9,8},{10,11... | collective-permute-start | bytes 3145736 | tf_op jit(solution)/shard_map/ppermute | solution.py:24
  250.9 5.4 %copy-start.34 = (bf16[1024,2048]{1,0:T(8,128)(2,1)S(1)}, bf16[1024,2048]{1,0:T(8,128)(2,1)}, u32[]{:S(2)}) copy-start(bf16[1024,2048]{1,0:T(8,128)(2,1)} %all-gather.5.cloned.1.call-done) | copy-start | bytes 12582916
  250.9 5.4 %copy-start.38 = (bf16[1024,2048]{1,0:T(8,128)(2,1)S(1)}, bf16[1024,2048]{1,0:T(8,128)(2,1)}, u32[]{:S(2)}) copy-start(bf16[1024,2048]{1,0:T(8,128)(2,1)} %copy-done.37) | copy-start | bytes 12582916
  277.4 7.8 %copy-start.12 = (bf16[16,8,8,512]{3,2,0,1:T(8,128)(2,1)S(1)}, bf16[16,8,8,512]{3,2,0,1:T(8,128)(2,1)}, u32[]{:S(2)}) copy-start(bf16[16,8,8,512]{3,2,0,1:T(8,128)(2,1)} %fusion.75) | copy-start | bytes 3145732
  278.5 42.4 %all-to-all-start.6 = ((bf16[16,8,8,512]{3,2,1,0:T(8,128)(2,1)}), bf16[16,8,8,512]{3,2,1,0:T(8,128)(2,1)S(1)}, u32[]{:S(2)}, u32[]{:S(2)}) async-start(bf16[16,8,8,512]{3,2,1,0:T(8,128)(2,1)} %copy.56), calls=%async_computation.6 | async-start | bytes 2097152 | tf_op jit(solution)/shard_map/all_to_all | solution.py:45
  320.9 40.7 %all-to-all-start.4 = ((bf16[16,8,8,512]{3,2,1,0:T(8,128)(2,1)}), bf16[16,8,8,512]{3,2,1,0:T(8,128)(2,1)S(1)}, u32[]{:S(2)}, u32[]{:S(2)}) async-start(bf16[16,8,8,512]{3,2,1,0:T(8,128)(2,1)} %copy.52), calls=%async_computation.4 | async-start | bytes 2097152 | tf_op jit(solution)/shard_map/all_to_all | solution.py:45
  328.5 7.2 %copy-start.20 = (bf16[1024,512]{1,0:T(8,128)(2,1)S(1)}, bf16[1024,512]{1,0:T(8,128)(2,1)}, u32[]{:S(2)}) copy-start(bf16[1024,512]{1,0:T(8,128)(2,1)} %get-tuple-element.40) | copy-start | bytes 3145732
  328.5 7.2 %copy-start.22 = (bf16[1024,512]{1,0:T(8,128)(2,1)S(1)}, bf16[1024,512]{1,0:T(8,128)(2,1)}, u32[]{:S(2)}) copy-start(bf16[1024,512]{1,0:T(8,128)(2,1)} %get-tuple-element.41) | copy-start | bytes 3145732
  328.5 7.2 %copy-start.35 = (bf16[1024,2048]{1,0:T(8,128)(2,1)S(1)}, bf16[1024,2048]{1,0:T(8,128)(2,1)}, u32[]{:S(2)}) copy-start(bf16[1024,2048]{1,0:T(8,128)(2,1)} %get-tuple-element.30) | copy-start | bytes 12582916
  333.9 25.7 %collective-permute-start.5 = (bf16[1024,512]{1,0:T(8,128)(2,1)S(1)}, bf16[1024,512]{1,0:T(8,128)(2,1)S(1)}, u32[]{:S(2)}, u32[]{:S(2)}) collective-permute-start(bf16[1024,512]{1,0:T(8,128)(2,1)S(1)} %fusion.48), channel_id=1, source_target_pairs={{0,1},{1,0},{2,3},{3,2},{4,5},{5,4},{6,7},{7,6},{8,9},{9,8},{10,11... | collective-permute-start | bytes 3145736 | tf_op jit(solution)/shard_map/ppermute | solution.py:24
  360.6 7.0 %copy-start.18 = (bf16[1024,512]{1,0:T(8,128)(2,1)S(1)}, bf16[1024,512]{1,0:T(8,128)(2,1)}, u32[]{:S(2)}) copy-start(bf16[1024,512]{1,0:T(8,128)(2,1)} %get-tuple-element.34) | copy-start | bytes 3145732
  361.6 28.8 %all-to-all-start.7 = ((bf16[16,8,8,512]{3,2,1,0:T(8,128)(2,1)}), bf16[16,8,8,512]{3,2,1,0:T(8,128)(2,1)}, u32[]{:S(2)}, u32[]{:S(2)}) async-start(bf16[16,8,8,512]{3,2,1,0:T(8,128)(2,1)} %bitcast.127), calls=%async_computation.7 | async-start | bytes 2097152 | tf_op jit(solution)/shard_map/all_to_all | solution.py:45
  367.5 93.7 %reduce-scatter.5.cloned.1.call-start = ((), (), s32[]{:S(2)}) async-start(), calls=%async_computation.13 | async-start | bytes 4456448 | tf_op jit(solution)/shard_map/reduce_scatter | solution.py:112
  390.5 35.8 %all-to-all-start.5 = ((bf16[16,8,8,512]{3,2,1,0:T(8,128)(2,1)}), bf16[16,8,8,512]{3,2,1,0:T(8,128)(2,1)}, u32[]{:S(2)}, u32[]{:S(2)}) async-start(bf16[16,8,8,512]{3,2,1,0:T(8,128)(2,1)} %bitcast.128), calls=%async_computation.5 | async-start | bytes 2097152 | tf_op jit(solution)/shard_map/all_to_all | solution.py:45
  397.6 8.4 %copy-start.32 = (bf16[1024,2048]{1,0:T(8,128)(2,1)S(1)}, bf16[1024,2048]{1,0:T(8,128)(2,1)}, u32[]{:S(2)}) copy-start(bf16[1024,2048]{1,0:T(8,128)(2,1)} %all-gather.3.cloned.1.call-done) | copy-start | bytes 12582916
  397.7 8.4 %copy-start.36 = (bf16[1024,2048]{1,0:T(8,128)(2,1)S(1)}, bf16[1024,2048]{1,0:T(8,128)(2,1)}, u32[]{:S(2)}) copy-start(bf16[1024,2048]{1,0:T(8,128)(2,1)} %get-tuple-element.30) | copy-start | bytes 12582916
  404.4 5.4 %copy-start.39 = (bf16[1024,2048]{1,0:T(8,128)(2,1)S(1)}, bf16[1024,2048]{1,0:T(8,128)(2,1)}, u32[]{:S(2)}) copy-start(bf16[1024,2048]{1,0:T(8,128)(2,1)} %get-tuple-element.22) | copy-start | bytes 12582916
  404.4 25.8 %collective-permute-start.7 = (bf16[1024,512]{1,0:T(8,128)(2,1)}, bf16[1024,512]{1,0:T(8,128)(2,1)}, u32[]{:S(2)}, u32[]{:S(2)}) collective-permute-start(bf16[1024,512]{1,0:T(8,128)(2,1)} %fusion.51), channel_id=1, source_target_pairs={{0,1},{1,0},{2,3},{3,2},{4,5},{5,4},{6,7},{7,6},{8,9},{9,8},{10,11... | collective-permute-start | bytes 3145736 | tf_op jit(solution)/shard_map/ppermute | solution.py:24
  409.8 16.5 %copy-start.7 = (bf16[8,128,512]{2,1,0:T(8,128)(2,1)S(1)}, bf16[8,128,512]{2,1,0:T(8,128)(2,1)}, u32[]{:S(2)}) copy-start(bf16[8,128,512]{2,1,0:T(8,128)(2,1)} %get-tuple-element.48) | copy-start | bytes 3145732
  409.8 16.5 %copy-start.24 = (bf16[1024,512]{1,0:T(8,128)(2,1)S(1)}, bf16[1024,512]{1,0:T(8,128)(2,1)}, u32[]{:S(2)}) copy-start(bf16[1024,512]{1,0:T(8,128)(2,1)} %copy-done.23) | copy-start | bytes 3145732
  426.3 3.9 copy-start.17
  430.2 3.6 copy-start.28
  (13 other events, 25.3 us)
Sparse Core Ops, SparseCore 0:
  10.2 81.3 all-gather.2
  93.7 77.9 all-gather.4
  251.0 96.9 reduce-scatter.2
  379.2 81.9 reduce-scatter.4

commit v2 on v1

v2 whole, which is shorter than its diff:
```python
import jax
import jax.numpy as jnp
from jax import lax
from jax.sharding import PartitionSpec as P

BF = jnp.bfloat16
F32 = jnp.float32


def body(
    inputs, first_factor, second_factor, gate_scale, gate_bias, in_weight, out_weight, cotangent
):
    seq_count, tok_rows, chan = inputs.shape
    blocks, size, _ = first_factor.shape
    offs = second_factor.shape[0]
    owners = lax.axis_size("seq")
    groups = lax.axis_size("fsdp")
    mine = lax.axis_index("fsdp")
    width = chan * groups
    gain = gate_scale.reshape(1, 1, chan)
    shift = gate_bias.reshape(1, 1, chan)

    def swap(x):
        return lax.ppermute(x, "fsdp", [(0, 1), (1, 0)])

    def gather_cols(x):
        if groups != 2:
            return lax.all_gather(x, "fsdp", axis=1, tiled=True)
        return place(x, swap(x))

    def place(x, y):
        first = mine == 0
        return jnp.concatenate([jnp.where(first, x, y), jnp.where(first, y, x)], axis=1)

    def reduce_cols(left, weight, dims):
        if groups != 2:
            full = lax.dot_general(left, weight, dims, preferred_element_type=F32)
            got = lax.all_to_all(full, "fsdp", split_axis=1, concat_axis=0, tiled=True)
            return jnp.sum(got.reshape(groups, -1, chan), axis=0), None
        other = lax.dynamic_slice_in_dim(weight, (1 - mine) * chan, chan, 0)
        own = lax.dynamic_slice_in_dim(weight, mine * chan, chan, 0)
        sent = swap(lax.dot_general(left, other, dims, preferred_element_type=F32).astype(BF))
        kept = lax.dot_general(left, own, dims, preferred_element_type=F32)
        return kept, sent

    def exchange(x):
        return lax.all_to_all(x, "seq", split_axis=0, concat_axis=0, tiled=True)

    bar = lax.optimization_barrier
    nt = (((1,), (1,)), ((), ()))
    tn = (((0,), (0,)), ((), ()))
    seqs = range(seq_count)
    last = seq_count - 1
    both = jnp.stack([in_weight, out_weight.T], axis=0)
    both = lax.all_gather(both, "seq", axis=1, tiled=True)
    full_in, full_out = both[0], both[1]

    sources = [inputs[s].reshape(blocks, size, chan) for s in seqs]
    cots = [cotangent[s] for s in seqs]
    cot_all = [gather_cols(c) for c in cots]

    source = inputs.reshape(seq_count, blocks, size, chan)
    u = jnp.einsum("mkn,smnc->mksc", first_factor, source, preferred_element_type=F32)
    u = u.astype(BF).reshape(blocks, owners, offs, seq_count, chan).transpose(1, 3, 0, 2, 4)
    u, *cot_all = bar((exchange(u), *cot_all))
    turned = [u[:, s].reshape(owners * blocks, offs, chan) for s in seqs]
    mixes, seconds, mixed_all = [], [], []
    for s in seqs:
        w = jnp.einsum("kjm,mkc->kjc", second_factor, turned[s], preferred_element_type=F32)
        w = w.astype(BF).reshape(offs, owners, blocks, chan).transpose(1, 0, 2, 3)
        w = exchange(w)
        if s > 0:
            w, mixed_all[s - 1] = bar((w, mixed_all[s - 1]))
        w = bar(w.reshape(size, blocks, chan).transpose(1, 0, 2))
        gate = jax.nn.sigmoid(gain * sources[s].astype(F32) + shift)
        seconds.append(w)
        mixes.append((gate * w.astype(F32)).astype(BF).reshape(tok_rows, chan))
        if s < last or groups != 2:
            mixed_all.append(gather_cols(mixes[s]))
    swapped = swap(mixes[last]) if groups == 2 else None

    das, hs, sums = [], [], []
    for s in seqs:
        pre = jnp.dot(mixed_all[s], full_in, preferred_element_type=F32)
        dh = jnp.dot(cot_all[s], full_out, preferred_element_type=F32)
        sig = jax.nn.sigmoid(pre)
        hs.append((pre * sig).astype(BF))
        da = (dh * sig * (1.0 + pre * (1.0 - sig))).astype(BF)
        if s < last and groups == 2:
            da, swapped = bar((da, swapped))
            mixed_all.append(place(mixes[last], swapped))
        if s > 0 and groups == 2:
            kept, sent = sums[s - 1]
            da, sent = bar((da, sent))
            sums[s - 1] = kept, sent
        das.append(da)
        sums.append(reduce_cols(da, full_in, nt))

    out_term = sum(lax.dot_general(cot_all[s], hs[s], tn, preferred_element_type=F32) for s in seqs)
    out_term = out_term.astype(BF)
    if groups == 2:
        kept, sent = sums[last]
        sent, out_term = bar((sent, out_term))
        sums[last] = kept, sent
    grad_out = lax.psum_scatter(out_term, "seq", scatter_dimension=0, tiled=True)
    dms, dws, gates = [], [], []
    for s in seqs:
        gate = jax.nn.sigmoid(gain * sources[s].astype(F32) + shift)
        kept, sent = sums[s]
        dm = cots[s].astype(F32) + (kept if sent is None else kept + sent.astype(F32))
        dm = dm.astype(BF).reshape(blocks, size, chan)
        dw = (dm.astype(F32) * gate).astype(BF)
        dms.append(dm)
        gates.append(gate)
        dws.append(dw.reshape(blocks, owners, offs, chan).transpose(1, 0, 2, 3))
    dw = exchange(jnp.stack(dws, axis=1))
    in_term = sum(lax.dot_general(mixed_all[s], das[s], tn, preferred_element_type=F32) for s in seqs)
    dw, in_term = bar((dw, in_term.astype(BF)))
    scale = 1.0 / size
    grad_in = lax.psum_scatter(in_term, "seq", scatter_dimension=0, tiled=True)

    branches = [list(reduce_cols(hs[s], full_out, nt)) for s in seqs]
    dw = dw.transpose(1, 0, 2, 3, 4).reshape(seq_count, owners * blocks, offs, chan)
    du = jnp.einsum("kjm,sjkc->kmsc", second_factor, dw, preferred_element_type=F32)
    du = du.astype(BF).reshape(offs, owners, blocks, seq_count, chan).transpose(1, 3, 0, 2, 4)
    du = exchange(du)
    if groups == 2:
        du, *sents = bar((du, *[pair[1] for pair in branches]))
        branches = [[pair[0], sent] for pair, sent in zip(branches, sents)]
    grads, results = [], []
    for s in seqs:
        rows = du[:, s].reshape(size, blocks, chan)
        back = jnp.einsum("mkn,kmc->mnc", first_factor, rows, preferred_element_type=F32)
        gate = gates[s]
        gate_term = dms[s].astype(F32) * seconds[s].astype(F32) * gate * (1.0 - gate) * gain
        grads.append((back + gate_term).astype(BF).reshape(tok_rows, chan))
        kept, sent = branches[s]
        branch = kept if sent is None else kept + sent.astype(F32)
        results.append((mixes[s].astype(F32) + branch).astype(BF))
    return (
        jnp.stack(results),
        jnp.stack(grads),
        grad_in.astype(F32) * scale,
        grad_out.astype(F32).T * scale,
    )


def solution(mesh):
    in_specs = (
        P(None, "seq", "fsdp"),
        P("seq", None, None),
        P("seq", None, None),
        P("fsdp"),
        P("fsdp"),
        P("seq", "fsdp"),
        P("fsdp", "seq"),
        P(None, "seq", "fsdp"),
    )
    out_specs = (P(None, "seq", "fsdp"), P(None, "seq", "fsdp"), P("seq", "fsdp"), P("fsdp", "seq"))
    return jax.shard_map(body, mesh=mesh, in_specs=in_specs, out_specs=out_specs, check_vma=False)
```

time: 475 us -> 466 us (0.981)
  waiting for transfers between devices: 226 us -> 203 us
  local copies, waits for them, and re-layouts: 20.8 us -> 27.1 us
  starting transfers between devices: 65.2 us -> 71.2 us
    all_to_all x8 -> x5, waiting for transfers between devices: 143 us -> 71.2 us  [exchange(): return lax.all_to_all(x, 'seq', split_axis=0, concat_axis=0, tiled=True)]
    ppermute x8, waiting for transfers between devices: 65 us -> 119 us  [swap(): return lax.ppermute(x, 'fsdp', [(0, 1), (1, 0)])]
    reduce_scatter x1, waiting for transfers between devices: 16.8 us -> 0.01 us  [body(): lax.psum_scatter(out_term, 'seq', scatter_dimension=0, tiled=True)]
    reduce_scatter x1, waiting for transfers between devices: 0.01 us -> 12.5 us  [body(): grad_in = lax.psum_scatter(in_term, 'seq', scatter_dimension=0, tiled=True)]
    all_to_all x8 -> x5, starting transfers between devices: 55.3 us -> 61.7 us  [exchange(): return lax.all_to_all(x, 'seq', split_axis=0, concat_axis=0, tiled=True)]
    dot_general x8 -> x6, matrix products: 25.9 us -> 30.3 us  [the longest x2 21.4 us: body(): dh = jnp.dot(cot_all[s], full_out, preferred_element_type=F32)]
  transfers between devices with their start and end apart: 20 -> 16, of which waited for: 13 -> 11; matrix products, arithmetic and copies ran while one was open for 34% -> 32% of each run, Pallas kernels for 0% -> 0%
where the time goes in v2:
time: 466 us; the launch traced here: 457 us
  waiting for transfers between devices  203 us (44%)
  matrix products  114 us (24%)
  starting transfers between devices  71.2 us (15%)
  other arithmetic  27.5 us (6%)
  local copies, waits for them, and re-layouts  27.1 us (6%)
  between operations  14.7 us (3%)
    ppermute x8, waiting for transfers between devices, swap(): return lax.ppermute(x, 'fsdp', [(0, 1), (1, 0)])  119 us
    all_to_all x5, waiting for transfers between devices, exchange(): return lax.all_to_all(x, 'seq', split_axis=0, concat_axis=0, tiled=True)  71.2 us
    all_to_all x5, starting transfers between devices, exchange(): return lax.all_to_all(x, 'seq', split_axis=0, concat_axis=0, tiled=True)  61.7 us
    dot_general x2, matrix products, body(): dh = jnp.dot(cot_all[s], full_out, preferred_element_type=F32)  21.4 us
    dot_general x2, matrix products, body(): pre = jnp.dot(mixed_all[s], full_in, preferred_element_type=F32)  19.4 us
    dot_general x4, matrix products, reduce_cols(): kept = lax.dot_general(left, own, dims, preferred_element_type=F32)  17.8 us
    dot_general x2, matrix products, body(): lax.dot_general(cot_all[s], hs[s], tn, preferred_element_type=F32)  15.7 us
    dot_general x4, matrix products, reduce_cols(): lax.dot_general(left, other, dims, preferred_element_type=F32).astype(BF)  15.4 us
  transfers between devices with their start and end apart: 16, of which 11 were waited for; matrix products, arithmetic and copies ran while one was open for 32% of the time, Pallas kernels for 0%

profile of v2, /device:TPU:0, one launch (start us, length us, event | category | flops | bytes accessed | tf_op | source)
XLA Modules:
  0.0 457.3 jit_solution(6899416606976113803)
XLA Ops:
  7.2 1.9 pad_maximum_fusion.9
  9.2 2.4 convert_bitcast_fusion.1
  13.2 7.4 %all-to-all-start = ((bf16[16,2,8,8,512]{4,3,1,2,0:T(8,128)(2,1)}), bf16[16,2,8,8,512]{4,3,1,2,0:T(8,128)(2,1)S(1)}, u32[]{:S(2)}, u32[]{:S(2)}) async-start(bf16[16,2,8,8,512]{4,3,1,2,0:T(8,128)(2,1)} %bitcast.199), calls=%async_computation | async-start | bytes 4194304 | tf_op jit(solution)/shard_map/all_to_all | solution.py:47
  20.5 3.1 slice_bitcast_fusion
  25.7 24.1 %collective-permute-done = bf16[1024,512]{1,0:T(8,128)(2,1)S(1)} collective-permute-done((bf16[1024,512]{1,0:T(8,128)(2,1)}, bf16[1024,512]{1,0:T(8,128)(2,1)S(1)}, u32[]{:S(2)}, u32[]{:S(2)}) %collective-permute-start) | collective-permute-done | bytes 1048608 | tf_op jit(solution)/shard_map/ppermute | solution.py:24
  49.9 22.1 %collective-permute-done.1 = bf16[1024,512]{1,0:T(8,128)(2,1)} collective-permute-done((bf16[1024,512]{1,0:T(8,128)(2,1)}, bf16[1024,512]{1,0:T(8,128)(2,1)}, u32[]{:S(2)}, u32[]{:S(2)}) %collective-permute-start.1) | collective-permute-done | bytes 1048608 | tf_op jit(solution)/shard_map/ppermute | solution.py:24
  72.0 2.1 broadcast_select_fusion.5
  74.1 2.7 pad_maximum_fusion
  81.6 27.0 %all-to-all-start.1 = ((bf16[16,8,8,512]{3,2,1,0:T(8,128)(2,1)}), bf16[16,8,8,512]{3,2,1,0:T(8,128)(2,1)S(1)}, u32[]{:S(2)}, u32[]{:S(2)}) async-start(bf16[16,8,8,512]{3,2,1,0:T(8,128)(2,1)} %bitcast.189), calls=%async_computation.1 | async-start | bytes 2097152 | tf_op jit(solution)/shard_map/all_to_all | solution.py:47
  108.6 3.6 slice_convert_fusion
  114.2 25.0 %all-to-all-done.1 = bf16[16,8,8,512]{3,2,1,0:T(8,128)(2,1)S(1)} async-done(((bf16[16,8,8,512]{3,2,1,0:T(8,128)(2,1)}), bf16[16,8,8,512]{3,2,1,0:T(8,128)(2,1)S(1)}, u32[]{:S(2)}, u32[]{:S(2)}) %all-to-all-start.1) | async-done | bytes 1048608 | tf_op jit(solution)/shard_map/all_to_all | solution.py:47
  139.2 7.3 %all-to-all-start.2 = ((bf16[16,8,8,512]{3,2,1,0:T(8,128)(2,1)}), bf16[16,8,8,512]{3,2,1,0:T(8,128)(2,1)}, u32[]{:S(2)}, u32[]{:S(2)}) async-start(bf16[16,8,8,512]{3,2,1,0:T(8,128)(2,1)} %bitcast.187), calls=%async_computation.2 | async-start | bytes 2097152 | tf_op jit(solution)/shard_map/all_to_all | solution.py:47
  150.8 24.1 %collective-permute-done.2 = bf16[1024,512]{1,0:T(8,128)(2,1)} collective-permute-done((bf16[1024,512]{1,0:T(8,128)(2,1)S(1)}, bf16[1024,512]{1,0:T(8,128)(2,1)}, u32[]{:S(2)}, u32[]{:S(2)}) %collective-permute-start.2) | collective-permute-done | bytes 1048608 | tf_op jit(solution)/shard_map/ppermute | solution.py:24
  181.8 11.3 %multiply_convert_fusion.3 = (bf16[1024,2048]{1,0:T(8,128)(2,1)S(1)}, f32[1024,2048]{1,0:T(8,128)}) fusion(bf16[1024,1024]{1,0:T(8,128)(2,1)} %pad_maximum_fusion.2, bf16[2,1024,2048]{2,1,0:T(8,128)(2,1)} %all-gather.2.cloned.1.call-done), kind=kOutput, calls=%fused_computation.6 | convolution fusion | flops 4305453056 | bytes 18874368 | tf_op jit(solution)/shard_map/dot_general | solution.py:84
  193.1 11.4 %multiply_convert_fusion.2 = bf16[1024,2048]{1,0:T(8,128)(2,1)} fusion(f32[1024,2048]{1,0:T(8,128)} %get-tuple-element.61, bf16[1024,1024]{1,0:T(8,128)(2,1)S(1)} %copy-done.23, bf16[2,1024,2048]{2,1,0:T(8,128)(2,1)S(1)} %copy-done.6), kind=kOutput, calls=%fused_computation.5 | convolution fusion | flops 4313841664 | bytes 18874368 | tf_op jit(solution)/shard_map/dot_general | solution.py:85
  206.5 2.6 fusion.103
  209.1 2.6 copy-done.34
  211.8 2.4 fusion.50
  215.6 8.1 %multiply_convert_fusion = (bf16[1024,2048]{1,0:T(8,128)(2,1)}, f32[1024,2048]{1,0:T(8,128)}) fusion(bf16[2,1024,2048]{2,1,0:T(8,128)(2,1)S(1)} %copy-done.6, bf16[1024,512]{1,0:T(8,128)(2,1)S(1)} %get-tuple-element.45, bf16[1024,512]{1,0:T(8,128)(2,1)S(1)} %get-tuple-element.44), kind=kOutput, calls=%fused_computation.2 | convolution fusion | flops 4309647360 | bytes 18874368 | tf_op jit(solution)/shard_map/dot_general | solution.py:84
  223.7 10.0 %multiply_convert_fusion.1 = bf16[1024,2048]{1,0:T(8,128)(2,1)} fusion(f32[1024,2048]{1,0:T(8,128)} %get-tuple-element.59, bf16[1024,1024]{1,0:T(8,128)(2,1)S(1)} %copy-done.22, bf16[2,1024,2048]{2,1,0:T(8,128)(2,1)S(1)} %copy-done.6), kind=kOutput, calls=%fused_computation.3 | convolution fusion | flops 4313841664 | bytes 18874368 | tf_op jit(solution)/shard_map/dot_general | solution.py:85
  233.7 7.0 %fusion.106 = f32[1024,2048]{1,0:T(8,128)} fusion(bf16[1024,1024]{1,0:T(8,128)(2,1)S(1)} %copy-done.23, bf16[1024,2048]{1,0:T(8,128)(2,1)S(1)} %get-tuple-element.60), kind=kOutput, calls=%fused_computation.138 | convolution fusion | flops 4294967296 | bytes 14680064 | tf_op jit(solution)/shard_map/dot_general | solution.py:99
  240.8 3.3 fusion.53
  244.7 8.7 %add_convert_fusion.1 = bf16[1024,2048]{1,0:T(8,128)(2,1)} fusion(f32[1024,2048]{1,0:T(8,128)} %fusion.106, bf16[1024,1024]{1,0:T(8,128)(2,1)S(1)} %copy-done.22, bf16[1024,2048]{1,0:T(8,128)(2,1)S(1)} %copy-done.36), kind=kOutput, calls=%fused_computation.1 | convolution fusion | flops 4299161600 | bytes 18874368 | tf_op jit(solution)/shard_map/dot_general | solution.py:99
  253.4 14.5 %collective-permute-done.5 = bf16[1024,512]{1,0:T(8,128)(2,1)} collective-permute-done((bf16[1024,512]{1,0:T(8,128)(2,1)}, bf16[1024,512]{1,0:T(8,128)(2,1)}, u32[]{:S(2)}, u32[]{:S(2)}) %collective-permute-start.5) | collective-permute-done | bytes 1048608 | tf_op jit(solution)/shard_map/ppermute | solution.py:24
  267.9 5.9 %fusion.67 = f32[1024,512]{1,0:T(8,128)S(1)} fusion(bf16[1024,512]{1,0:T(8,128)(2,1)} %copy-done.29, bf16[1024,2048]{1,0:T(8,128)(2,1)} %multiply_convert_fusion.2, bf16[1,1024,2048]{2,1,0:T(8,128)(2,1)} %copy-done.14, s32[]{:T(128)S(6)} %select_n.55, bf16[2,1024,512]{2,1,0:T(8,128)(2,1)} %param.15), kind=kOutput, calls=%fused_computation.86 | convolution fusion | flops 2150629376 | bytes 10485764 | tf_op jit(solution)/shard_map/dot_general | solution.py:43
  274.5 4.5 fusion.72
  280.6 1.7 copy.48
  282.3 5.5 %all-to-all-start.3 = ((bf16[16,2,8,8,512]{4,3,2,1,0:T(8,128)(2,1)}), bf16[16,2,8,8,512]{4,3,2,1,0:T(8,128)(2,1)}, u32[]{:S(2)}, u32[]{:S(2)}) async-start(bf16[16,2,8,8,512]{4,3,2,1,0:T(8,128)(2,1)} %copy.48), calls=%async_computation.3 | async-start | bytes 4194304 | tf_op jit(solution)/shard_map/all_to_all | solution.py:47
  287.8 7.2 %fusion.64 = f32[1024,2048]{1,0:T(8,128)S(1)} fusion(bf16[1024,2048]{1,0:T(8,128)(2,1)} %multiply_convert_fusion.1, bf16[1024,512]{1,0:T(8,128)(2,1)} %copy-done.25, bf16[1024,512]{1,0:T(8,128)(2,1)} %copy-done.24), kind=kOutput, calls=%fused_computation.85 | convolution fusion | flops 4299161600 | bytes 14680064 | tf_op jit(solution)/shard_map/dot_general | solution.py:117
  295.0 6.2 %add_convert_fusion = bf16[1024,2048]{1,0:T(8,128)(2,1)} fusion(f32[1024,2048]{1,0:T(8,128)S(1)} %fusion.64, bf16[1024,1024]{1,0:T(8,128)(2,1)S(1)} %copy-done.19, bf16[1024,2048]{1,0:T(8,128)(2,1)S(1)} %copy-done.35), kind=kOutput, calls=%fused_computation | convolution fusion | flops 4299161600 | bytes 18874368 | tf_op jit(solution)/shard_map/dot_general | solution.py:117
  301.2 44.5 %all-to-all-done.3 = bf16[16,2,8,8,512]{4,3,2,1,0:T(8,128)(2,1)} async-done(((bf16[16,2,8,8,512]{4,3,2,1,0:T(8,128)(2,1)}), bf16[16,2,8,8,512]{4,3,2,1,0:T(8,128)(2,1)}, u32[]{:S(2)}, u32[]{:S(2)}) %all-to-all-start.3) | async-done | bytes 2097184 | tf_op jit(solution)/shard_map/all_to_all | solution.py:47
  345.7 1.7 copy.49
  347.5 1.6 convert_bitcast_fusion
  350.8 14.5 %all-to-all-start.4 = ((bf16[16,2,8,8,512]{4,3,1,2,0:T(8,128)(2,1)}), bf16[16,2,8,8,512]{4,3,1,2,0:T(8,128)(2,1)}, u32[]{:S(2)}, u32[]{:S(2)}) async-start(bf16[16,2,8,8,512]{4,3,1,2,0:T(8,128)(2,1)} %bitcast.200), calls=%async_computation.4 | async-start | bytes 4194304 | tf_op jit(solution)/shard_map/all_to_all | solution.py:47
  366.1 6.4 %fusion.59 = bf16[1024,512]{1,0:T(8,128)(2,1)} fusion(bf16[1024,2048]{1,0:T(8,128)(2,1)} %get-tuple-element.58, bf16[1,1024,2048]{2,1,0:T(8,128)(2,1)} %get-tuple-element.37, s32[]{:T(128)S(6)} %select_n.58), kind=kOutput, calls=%fused_computation.80 | convolution fusion | flops 2148007936 | bytes 7340036 | tf_op jit(solution)/shard_map/dot_general | solution.py:42
  372.6 3.3 fusion.56
  375.9 1.9 collective-permute-start.6
  377.8 3.7 fusion.32
  381.5 3.7 fusion.30
  385.2 1.8 multiply_bitcast_fusion
  387.0 11.8 %collective-permute-done.7 = bf16[1024,512]{1,0:T(8,128)(2,1)} collective-permute-done((bf16[1024,512]{1,0:T(8,128)(2,1)}, bf16[1024,512]{1,0:T(8,128)(2,1)}, u32[]{:S(2)}, u32[]{:S(2)}) %collective-permute-start.7) | collective-permute-done | bytes 1048608 | tf_op jit(solution)/shard_map/ppermute | solution.py:24
  398.7 21.9 %collective-permute-done.6 = bf16[1024,512]{1,0:T(8,128)(2,1)} collective-permute-done((bf16[1024,512]{1,0:T(8,128)(2,1)}, bf16[1024,512]{1,0:T(8,128)(2,1)}, u32[]{:S(2)}, u32[]{:S(2)}) %collective-permute-start.6) | collective-permute-done | bytes 1048608 | tf_op jit(solution)/shard_map/ppermute | solution.py:24
  420.6 1.9 fusion.104
  423.2 3.3 fusion.11
  430.9 1.8 fusion.75
  432.8 1.7 fusion.76
  436.0 12.5 %reduce-scatter.3.cloned.1.call-done = bf16[64,2048]{1,0:T(8,128)(2,1)} async-done(((bf16[1024,2048]{1,0:T(8,128)(2,1)}), bf16[64,2048]{1,0:T(8,128)(2,1)}) %reduce-scatter.3.cloned.1.call-update) | async-done | bytes 262160 | tf_op jit(solution)/shard_map/reduce_scatter | solution.py:120
  448.5 1.8 convert_multiply_fusion.4
  (114 shorter events, 36.9 us)
Async XLA Ops:
  7.2 72.4 %copy-start = (bf16[8,128,128]{2,1,0:T(8,128)(2,1)S(1)}, bf16[8,128,128]{2,1,0:T(8,128)(2,1)}, u32[]{:S(2)}) copy-start(bf16[8,128,128]{2,1,0:T(8,128)(2,1)} %param.10) | copy-start | bytes 786436
  7.2 174.6 %all-gather.2.cloned.1.call-start = ((), (), s32[]{:S(2)}) async-start(), calls=%async_computation.7 | async-start | bytes 8912896 | tf_op jit(solution)/shard_map/all_gather | solution.py:55
  13.2 65.2 %all-to-all-start = ((bf16[16,2,8,8,512]{4,3,1,2,0:T(8,128)(2,1)}), bf16[16,2,8,8,512]{4,3,1,2,0:T(8,128)(2,1)S(1)}, u32[]{:S(2)}, u32[]{:S(2)}) async-start(bf16[16,2,8,8,512]{4,3,1,2,0:T(8,128)(2,1)} %bitcast.199), calls=%async_computation | async-start | bytes 4194304 | tf_op jit(solution)/shard_map/all_to_all | solution.py:47
  23.7 26.2 %collective-permute-start = (bf16[1024,512]{1,0:T(8,128)(2,1)}, bf16[1024,512]{1,0:T(8,128)(2,1)S(1)}, u32[]{:S(2)}, u32[]{:S(2)}) collective-permute-start(bf16[1024,512]{1,0:T(8,128)(2,1)} %get-tuple-element.55), channel_id=1, source_target_pairs={{0,1},{1,0},{2,3},{3,2},{4,5},{5,4},{6,7},{7,6},{8,9},{9,8},{10,11... | collective-permute-start | bytes 3145736 | tf_op jit(solution)/shard_map/ppermute | solution.py:24
  25.2 46.8 %collective-permute-start.1 = (bf16[1024,512]{1,0:T(8,128)(2,1)}, bf16[1024,512]{1,0:T(8,128)(2,1)}, u32[]{:S(2)}, u32[]{:S(2)}) collective-permute-start(bf16[1024,512]{1,0:T(8,128)(2,1)} %get-tuple-element.54), channel_id=1, source_target_pairs={{0,1},{1,0},{2,3},{3,2},{4,5},{5,4},{6,7},{7,6},{8,9},{9,8},{10,11... | collective-permute-start | bytes 3145736 | tf_op jit(solution)/shard_map/ppermute | solution.py:24
  81.6 57.6 %all-to-all-start.1 = ((bf16[16,8,8,512]{3,2,1,0:T(8,128)(2,1)}), bf16[16,8,8,512]{3,2,1,0:T(8,128)(2,1)S(1)}, u32[]{:S(2)}, u32[]{:S(2)}) async-start(bf16[16,8,8,512]{3,2,1,0:T(8,128)(2,1)} %bitcast.189), calls=%async_computation.1 | async-start | bytes 2097152 | tf_op jit(solution)/shard_map/all_to_all | solution.py:47
  108.6 3.6 copy-start.12
  139.2 7.7 %copy-start.27 = (f32[512]{0:T(512)S(1)}, f32[512]{0:T(512)}, u32[]{:S(2)}) copy-start(f32[512]{0:T(512)} %param.12) | copy-start | bytes 6148
  139.2 7.7 %copy-start.28 = (f32[512]{0:T(512)S(1)}, f32[512]{0:T(512)}, u32[]{:S(2)}) copy-start(f32[512]{0:T(512)} %param.11) | copy-start | bytes 6148
  139.2 38.6 %all-to-all-start.2 = ((bf16[16,8,8,512]{3,2,1,0:T(8,128)(2,1)}), bf16[16,8,8,512]{3,2,1,0:T(8,128)(2,1)}, u32[]{:S(2)}, u32[]{:S(2)}) async-start(bf16[16,8,8,512]{3,2,1,0:T(8,128)(2,1)} %bitcast.187), calls=%async_computation.2 | async-start | bytes 2097152 | tf_op jit(solution)/shard_map/all_to_all | solution.py:47
  146.6 238.6 %reduce-scatter.5.cloned.1.call-start = ((), (), s32[]{:S(2)}) async-start(), calls=%async_computation.9 | async-start | bytes 4456448 | tf_op jit(solution)/shard_map/reduce_scatter | solution.py:105
  146.9 2.3 copy-start.8
  149.3 27.0 %copy-start.4 = (bf16[8,128,512]{2,1,0:T(8,128)(2,1)}, bf16[8,128,512]{2,1,0:T(8,128)(2,1)S(1)}, u32[]{:S(2)}) copy-start(bf16[8,128,512]{2,1,0:T(8,128)(2,1)S(1)} %fusion.6) | copy-start | bytes 3145732
  149.3 25.6 %collective-permute-start.2 = (bf16[1024,512]{1,0:T(8,128)(2,1)S(1)}, bf16[1024,512]{1,0:T(8,128)(2,1)}, u32[]{:S(2)}, u32[]{:S(2)}) collective-permute-start(bf16[1024,512]{1,0:T(8,128)(2,1)S(1)} %bitcast.196), channel_id=1, source_target_pairs={{0,1},{1,0},{2,3},{3,2},{4,5},{5,4},{6,7},{7,6},{8,9},{9,8},{10,11... | collective-permute-start | bytes 3145736 | tf_op jit(solution)/shard_map/ppermute | solution.py:24
  180.4 24.7 %collective-permute-start.3 = (bf16[1024,512]{1,0:T(8,128)(2,1)S(1)}, bf16[1024,512]{1,0:T(8,128)(2,1)}, u32[]{:S(2)}, u32[]{:S(2)}) collective-permute-start(bf16[1024,512]{1,0:T(8,128)(2,1)S(1)} %bitcast.197), channel_id=1, source_target_pairs={{0,1},{1,0},{2,3},{3,2},{4,5},{5,4},{6,7},{7,6},{8,9},{9,8},{10,11... | collective-permute-start | bytes 3145736 | tf_op jit(solution)/shard_map/ppermute | solution.py:24
  181.8 11.3 %copy-start.6 = (bf16[2,1024,2048]{2,1,0:T(8,128)(2,1)S(1)}, bf16[2,1024,2048]{2,1,0:T(8,128)(2,1)}, u32[]{:S(2)}) copy-start(bf16[2,1024,2048]{2,1,0:T(8,128)(2,1)} %all-gather.2.cloned.1.call-done) | copy-start | bytes 25165828
  181.8 11.3 %copy-start.23 = (bf16[1024,1024]{1,0:T(8,128)(2,1)S(1)}, bf16[1024,1024]{1,0:T(8,128)(2,1)}, u32[]{:S(2)}) copy-start(bf16[1024,1024]{1,0:T(8,128)(2,1)} %get-tuple-element.22) | copy-start | bytes 6291460
  193.1 40.6 %copy-start.30 = (bf16[1024,2048]{1,0:T(8,128)(2,1)}, bf16[1024,2048]{1,0:T(8,128)(2,1)S(1)}, u32[]{:S(2)}) copy-start(bf16[1024,2048]{1,0:T(8,128)(2,1)S(1)} %get-tuple-element.60) | copy-start | bytes 12582916
  206.5 9.2 %copy-start.24 = (bf16[1024,512]{1,0:T(8,128)(2,1)}, bf16[1024,512]{1,0:T(8,128)(2,1)S(1)}, u32[]{:S(2)}) copy-start(bf16[1024,512]{1,0:T(8,128)(2,1)S(1)} %get-tuple-element.44) | copy-start | bytes 3145732
  206.5 9.2 %copy-start.25 = (bf16[1024,512]{1,0:T(8,128)(2,1)}, bf16[1024,512]{1,0:T(8,128)(2,1)S(1)}, u32[]{:S(2)}) copy-start(bf16[1024,512]{1,0:T(8,128)(2,1)S(1)} %get-tuple-element.45) | copy-start | bytes 3145732
  206.5 5.3 %copy-start.34 = (bf16[1024,2048]{1,0:T(8,128)(2,1)S(1)}, bf16[1024,2048]{1,0:T(8,128)(2,1)}, u32[]{:S(2)}) copy-start(bf16[1024,2048]{1,0:T(8,128)(2,1)} %multiply_convert_fusion.2) | copy-start | bytes 12582916
  209.1 31.6 %copy-start.14 = (bf16[1,1024,2048]{2,1,0:T(8,128)(2,1)}, bf16[1,1024,2048]{2,1,0:T(8,128)(2,1)S(1)}, u32[]{:S(2)}) copy-start(bf16[1,1024,2048]{2,1,0:T(8,128)(2,1)S(1)} %get-tuple-element.36) | copy-start | bytes 12582916
  214.1 26.6 %collective-permute-start.4 = (bf16[1024,512]{1,0:T(8,128)(2,1)S(1)}, bf16[1024,512]{1,0:T(8,128)(2,1)S(1)}, u32[]{:S(2)}, u32[]{:S(2)}) collective-permute-start(bf16[1024,512]{1,0:T(8,128)(2,1)S(1)} %fusion.50), channel_id=1, source_target_pairs={{0,1},{1,0},{2,3},{3,2},{4,5},{5,4},{6,7},{7,6},{8,9},{9,8},{10,11... | collective-permute-start | bytes 3145736 | tf_op jit(solution)/shard_map/ppermute | solution.py:24
  215.6 8.1 %copy-start.22 = (bf16[1024,1024]{1,0:T(8,128)(2,1)S(1)}, bf16[1024,1024]{1,0:T(8,128)(2,1)}, u32[]{:S(2)}) copy-start(bf16[1024,1024]{1,0:T(8,128)(2,1)} %get-tuple-element.25) | copy-start | bytes 6291460
  233.7 7.0 %copy-start.32 = (bf16[1024,2048]{1,0:T(8,128)(2,1)S(1)}, bf16[1024,2048]{1,0:T(8,128)(2,1)}, u32[]{:S(2)}) copy-start(bf16[1024,2048]{1,0:T(8,128)(2,1)} %multiply_convert_fusion.1) | copy-start | bytes 12582916
  240.7 4.0 copy-start.36
  240.8 3.3 copy-start.29
  244.1 23.7 %collective-permute-start.5 = (bf16[1024,512]{1,0:T(8,128)(2,1)}, bf16[1024,512]{1,0:T(8,128)(2,1)}, u32[]{:S(2)}, u32[]{:S(2)}) collective-permute-start(bf16[1024,512]{1,0:T(8,128)(2,1)} %fusion.53), channel_id=1, source_target_pairs={{0,1},{1,0},{2,3},{3,2},{4,5},{5,4},{6,7},{7,6},{8,9},{9,8},{10,11... | collective-permute-start | bytes 3145736 | tf_op jit(solution)/shard_map/ppermute | solution.py:24
  267.9 5.9 %copy-start.7 = (bf16[2,1024,512]{2,1,0:T(8,128)(2,1)S(1)}, bf16[2,1024,512]{2,1,0:T(8,128)(2,1)}, u32[]{:S(2)}) copy-start(bf16[2,1024,512]{2,1,0:T(8,128)(2,1)} %param.15) | copy-start | bytes 6291460
  267.9 5.9 %copy-start.15 = (bf16[1,1024,2048]{2,1,0:T(8,128)(2,1)S(1)}, bf16[1,1024,2048]{2,1,0:T(8,128)(2,1)}, u32[]{:S(2)}) copy-start(bf16[1,1024,2048]{2,1,0:T(8,128)(2,1)} %copy-done.14) | copy-start | bytes 12582916
  267.9 6.6 %copy-start.33 = (bf16[1024,2048]{1,0:T(8,128)(2,1)S(1)}, bf16[1024,2048]{1,0:T(8,128)(2,1)}, u32[]{:S(2)}) copy-start(bf16[1024,2048]{1,0:T(8,128)(2,1)} %multiply_convert_fusion.1) | copy-start | bytes 12582916
  274.5 4.6 copy-start.18
  274.5 4.6 copy-start.2
  282.3 63.5 %all-to-all-start.3 = ((bf16[16,2,8,8,512]{4,3,2,1,0:T(8,128)(2,1)}), bf16[16,2,8,8,512]{4,3,2,1,0:T(8,128)(2,1)}, u32[]{:S(2)}, u32[]{:S(2)}) async-start(bf16[16,2,8,8,512]{4,3,2,1,0:T(8,128)(2,1)} %copy.48), calls=%async_computation.3 | async-start | bytes 4194304 | tf_op jit(solution)/shard_map/all_to_all | solution.py:47
  287.8 7.2 %copy-start.19 = (bf16[1024,1024]{1,0:T(8,128)(2,1)S(1)}, bf16[1024,1024]{1,0:T(8,128)(2,1)}, u32[]{:S(2)}) copy-start(bf16[1024,1024]{1,0:T(8,128)(2,1)} %pad_maximum_fusion.2) | copy-start | bytes 6291460
  287.8 7.2 %copy-start.35 = (bf16[1024,2048]{1,0:T(8,128)(2,1)S(1)}, bf16[1024,2048]{1,0:T(8,128)(2,1)}, u32[]{:S(2)}) copy-start(bf16[1024,2048]{1,0:T(8,128)(2,1)} %multiply_convert_fusion.2) | copy-start | bytes 12582916
  350.8 69.9 %all-to-all-start.4 = ((bf16[16,2,8,8,512]{4,3,1,2,0:T(8,128)(2,1)}), bf16[16,2,8,8,512]{4,3,1,2,0:T(8,128)(2,1)}, u32[]{:S(2)}, u32[]{:S(2)}) async-start(bf16[16,2,8,8,512]{4,3,1,2,0:T(8,128)(2,1)} %bitcast.200), calls=%async_computation.4 | async-start | bytes 4194304 | tf_op jit(solution)/shard_map/all_to_all | solution.py:47
  365.3 83.2 %reduce-scatter.3.cloned.1.call-start = ((), (), s32[]{:S(2)}) async-start(), calls=%async_computation.8 | async-start | bytes 4456448 | tf_op jit(solution)/shard_map/reduce_scatter | solution.py:120
  366.0 6.5 %copy-start.13 = (bf16[1,1024,2048]{2,1,0:T(8,128)(2,1)S(1)}, bf16[1,1024,2048]{2,1,0:T(8,128)(2,1)}, u32[]{:S(2)}) copy-start(bf16[1,1024,2048]{2,1,0:T(8,128)(2,1)} %get-tuple-element.37) | copy-start | bytes 12582916
  366.0 6.5 %copy-start.31 = (bf16[1024,2048]{1,0:T(8,128)(2,1)S(1)}, bf16[1024,2048]{1,0:T(8,128)(2,1)}, u32[]{:S(2)}) copy-start(bf16[1024,2048]{1,0:T(8,128)(2,1)} %copy-done.30) | copy-start | bytes 12582916
  372.4 26.3 %collective-permute-start.7 = (bf16[1024,512]{1,0:T(8,128)(2,1)}, bf16[1024,512]{1,0:T(8,128)(2,1)}, u32[]{:S(2)}, u32[]{:S(2)}) collective-permute-start(bf16[1024,512]{1,0:T(8,128)(2,1)} %fusion.59), channel_id=1, source_target_pairs={{0,1},{1,0},{2,3},{3,2},{4,5},{5,4},{6,7},{7,6},{8,9},{9,8},{10,11... | collective-permute-start | bytes 3145736 | tf_op jit(solution)/shard_map/ppermute | solution.py:24
  375.9 5.6 %copy-start.37 = (bf16[1024,2048]{1,0:T(8,128)(2,1)S(1)}, bf16[1024,2048]{1,0:T(8,128)(2,1)}, u32[]{:S(2)}) copy-start(bf16[1024,2048]{1,0:T(8,128)(2,1)} %get-tuple-element.58) | copy-start | bytes 12582916
  375.9 44.7 %collective-permute-start.6 = (bf16[1024,512]{1,0:T(8,128)(2,1)}, bf16[1024,512]{1,0:T(8,128)(2,1)}, u32[]{:S(2)}, u32[]{:S(2)}) collective-permute-start(bf16[1024,512]{1,0:T(8,128)(2,1)} %fusion.56), channel_id=1, source_target_pairs={{0,1},{1,0},{2,3},{3,2},{4,5},{5,4},{6,7},{7,6},{8,9},{9,8},{10,11... | collective-permute-start | bytes 3145736 | tf_op jit(solution)/shard_map/ppermute | solution.py:24
  420.6 2.6 copy-start.9
  420.6 2.6 copy-start.26
  423.2 3.4 copy-start.11
  423.2 3.4 copy-start.17
  428.2 2.7 copy-start.21
  (6 other events, 10.0 us)
Sparse Core Ops, SparseCore 0:
  10.8 127.3 all-gather.1
  268.0 96.6 reduce-scatter.4
  370.5 77.9 reduce-scatter.2
